TPU v7x, 256 devices: a whole 4x4x8 slice. The times are simulated.
256 devices in a mesh: gx: 32 (over y_hi, z, core), gy: 8 (over x, y_lo).
Axes of the slice: x: 4, y: 4 (y_hi: 2, y_lo: 2; y = y_hi * 2 + y_lo), z: 8, core: 2. Of those that a mesh axis runs over, the one named last changes fastest.
Arguments:
- charge: float32 [1024, 8192], P('gx', 'gy'), may hold values from -8 to 8
Outputs:
- potential: float32 [1024, 8192], P('gx', 'gy')
All inputs are finite; a program needn't handle non-finite values.
Results may differ from a plain program's by a relative error of at most 0.0003.
Values sent between devices are 32-bit elements; how exact they have to be, the bound alone decides.
No kernel may reach another device: no remote copies, remote signals or barrier semaphores. Data moves between devices by JAX's collectives and lax.ppermute only.
A program may use at most 128 MiB of HBM per device.

v0:
```python
import functools

import jax
import jax.numpy as jnp
import ml_dtypes
import numpy as np
from jax import lax
from jax.experimental import pallas as pl
from jax.experimental.pallas import tpu as pltpu
from jax.sharding import PartitionSpec as P

P_SIZE = 32
W = 16
Q = 4
NL = 16
N_GX = 32
N_GY = 8
CELLS = P_SIZE // Q
VMEM_LIMIT = 56 * 1024 * 1024
BF16 = jnp.bfloat16
F32 = jnp.float32


def sine(length):
    counter = np.arange(length) + 1
    multiple = counter[:, None] * counter[None, :] % (2 * (length + 1))
    return np.sin(np.pi * multiple / (length + 1))


def eigen(length):
    return 2.0 - 2.0 * np.cos(np.pi * (np.arange(length) + 1) / (length + 1))


def interp(fine_start, fine_count, coarse_start, coarse_count, ratio):
    fine_pos = np.arange(fine_count) + fine_start
    coarse_pos = np.arange(coarse_count) + coarse_start
    numerator = 2 * fine_pos - (ratio - 1)
    lower_index = numerator // (2 * ratio)
    weight = ((numerator - 2 * ratio * lower_index) / (2.0 * ratio))[:, None]
    below = (coarse_pos[None, :] == lower_index[:, None]).astype(np.float64)
    above = (coarse_pos[None, :] == lower_index[:, None] + 1).astype(np.float64)
    return below * (1.0 - weight) + above * weight


def legendre(length, count):
    points = (2.0 * np.arange(length) + 1.0) / length - 1.0
    columns = [np.ones_like(points), points]
    for degree in range(2, count):
        columns.append(
            ((2 * degree - 1) * points * columns[-1] - (degree - 1) * columns[-2]) / degree
        )
    result = []
    for column in columns[:count]:
        vector = column
        for _ in range(2):
            for earlier in result:
                vector = vector - np.sum(earlier * vector) * earlier
        result.append(vector / np.sqrt(np.sum(vector * vector)))
    return np.stack(result, axis=1)


def columns_at(table, positions):
    positions = np.asarray(positions)
    inside = (positions >= 0) & (positions < table.shape[1])
    return table[:, np.clip(positions, 0, table.shape[1] - 1)] * inside


def pair(table):
    table = np.asarray(table, np.float64)
    high = table.astype(np.float32).astype(ml_dtypes.bfloat16)
    low = (table - high.astype(np.float64)).astype(np.float32).astype(ml_dtypes.bfloat16)
    return np.stack([high, low], axis=-3)


@functools.lru_cache(None)
def tables():
    t = {}
    n = P_SIZE + 2 * W
    s64, m64 = sine(n), eigen(n)
    s32, m32 = sine(P_SIZE), eigen(P_SIZE)
    s8, m8 = sine(CELLS), eigen(CELLS)
    nx, ny = CELLS * N_GX, CELLS * N_GY
    sx, mx = sine(nx), eigen(nx)
    sy, my = sine(ny), eigen(ny)
    eye = np.eye
    basis = legendre(P_SIZE, NL)
    fine = interp(0, n, 0, n // Q, Q)
    mean = np.kron(eye(n // Q), np.full((1, Q), 1.0 / Q))
    inside = slice(W, W + P_SIZE)
    places = [W - 1, W + P_SIZE, W, W + P_SIZE - 1]
    r = mean @ s64
    bs = basis.T @ s64[inside]
    st = s64[places]
    bl = basis.T @ fine[inside]
    lt = fine[places]
    slot_x, slot_y = [0, 1, 4, 5], [2, 3, 6, 7]
    sc = s64[:, inside]
    t["sc"] = pair(sc)
    t["bd"] = pair(np.kron(eye(4), sc.T))
    kx = m64.reshape(16, 1, 4, 1)
    rm = (2.0 / (n + 1)) ** 3 / (kx + m64.reshape(1, n, 1, 1) + m64.reshape(1, 1, 1, n))
    t["rm"] = rm.reshape(16 * n, 4 * n).astype(np.float32)
    ty = np.zeros((4, n, 256))
    for i in range(4):
        ty[i, :, i * 16 : i * 16 + 16] = r.T
        ty[i, :, 64 + i * 16 : 64 + i * 16 + 16] = bs.T
        ty[i, :, 128 + i * 4 : 128 + i * 4 + 4] = st.T
    t["ty"] = pair(ty.reshape(4 * n, 256))
    t["tz"] = pair(np.kron(eye(4), np.concatenate([r, bs], axis=0)))
    t["tx1"] = pair(np.kron(r.T, eye(16)))
    tx2 = np.zeros((n, NL, 8, NL))
    tx3 = np.zeros((n, 4, 8, NL))
    kl = np.zeros((16, 16, 8, NL))
    for i in range(4):
        tx2[:, :, slot_x[i], :] = st[i][:, None, None] * eye(NL)
        tx3[:, i, slot_y[i], :] = bs.T
        kl[:, :, slot_x[i], :] = lt[i][:, None, None] * bl.T[None]
        kl[:, :, slot_y[i], :] = bl.T[:, None, :] * lt[i][None, :, None]
    t["tx2"] = pair(tx2.reshape(n * NL, 128))
    t["tx3"] = pair(tx3.reshape(n * 4, 128))
    t["kl"] = pair(kl.reshape(256, 128))
    first = W // Q
    u1 = np.zeros((CELLS, 16))
    u2 = np.zeros((CELLS, 16))
    for k in range(CELLS):
        u1[:, k + first] += s8[:, k]
        u2[:, k + first - 1] -= s8[:, k] / (Q * Q)
        u2[:, k + first + 1] -= s8[:, k] / (Q * Q)
    t["u"] = pair(np.concatenate([u1, u2, bl], axis=0))
    beside = eye(16, k=1) + eye(16, k=-1)
    k1 = 6.0 * eye(256) - np.kron(beside, eye(16)) - np.kron(eye(16), beside)
    t["k1"] = pair(k1 / (Q * Q))
    tb = [np.tile(columns_at(sy, np.arange(16) + b * CELLS - first).T, (1, CELLS)) for b in range(N_GY)]
    t["tb"] = pair(np.stack(tb))
    ta = [np.repeat(columns_at(sx, np.arange(16) + a * CELLS - first), CELLS, axis=1) for a in range(N_GX)]
    t["ta"] = pair(np.stack(ta))
    scale = Q * Q * (2.0 / (nx + 1)) * (2.0 / (ny + 1)) * (2.0 / (CELLS + 1))
    wc = scale / (mx.reshape(nx, 1, 1) + m8.reshape(1, CELLS, 1) + my.reshape(1, 1, ny))
    t["wc"] = wc.reshape(nx, CELLS * ny).astype(np.float32)
    edge = interp(-1, P_SIZE + 2, -1, CELLS + 2, Q)
    ends = edge[[0, P_SIZE + 1]]
    lateral = edge[1 : P_SIZE + 1]
    depth = interp(0, P_SIZE, 0, CELLS, Q)
    around = np.arange(CELLS + 2) - 1
    y_near = np.stack([columns_at(sy, around + b * CELLS) for b in range(N_GY)], axis=1)
    x_near = np.stack([columns_at(sx, around + a * CELLS) for a in range(N_GX)], axis=1)
    tf = np.zeros((CELLS, ny, N_GY, 2, CELLS))
    tc = np.zeros((4, ny, N_GY, 16, 4))
    y_ends = np.einsum("fe,ybe->ybf", ends, y_near)
    for k in range(CELLS):
        tf[k, :, :, :, k] = y_ends
    for k in range(4):
        tc[k, :, :, : CELLS + 2, k] = y_near
    t["tf"] = pair(tf.reshape(CELLS * ny, 128))
    t["tc"] = pair(tc.reshape(4 * ny, 512))
    t["ec"] = pair(x_near.transpose(2, 1, 0).reshape((CELLS + 2) * N_GX, nx))
    t["ef"] = pair(np.einsum("fe,xae->fax", ends, x_near).reshape(2 * N_GX, nx))
    t["s32"] = pair(s32)
    t["bd32"] = pair(np.kron(eye(4), s32))
    rm32 = m32.reshape(8, 1, 4, 1) + m32.reshape(1, 32, 1, 1) + m32.reshape(1, 1, 1, 32)
    t["rm32"] = ((2.0 / (P_SIZE + 1)) ** 3 / rm32).reshape(256, 128).astype(np.float32)
    t["sbz"] = pair(s32 @ basis)
    lz = s32 @ depth @ s8
    lane = np.arange(128)
    t["lz"] = np.stack([lz[:, lane // 64 * 4 + lane % 4], lz[:, lane % 8]]).astype(np.float32)
    sel = np.zeros((N_GY, 4, 128, 128), np.float32)
    for b in range(N_GY):
        for f in range(2):
            for i in range(128):
                where_x = i % 64 // 4
                where_y = (i // 8 - 2 * b - f) % 16
                if where_x < CELLS + 2:
                    sel[b, f, i, 64 + f * 16 + where_x] = 1.0
                if where_y < CELLS + 2:
                    sel[b, 2 + f, i, 96 + f * 16 + where_y] = 1.0
    t["sel"] = sel.reshape(N_GY, 512, 128).astype(ml_dtypes.bfloat16)
    tz2 = np.zeros((128, 32, 32))
    sb, sl = s32 @ basis, s32 @ lateral
    for f, layer in enumerate([0, P_SIZE - 1]):
        near = s32[:, layer]
        for i in range(NL):
            tz2[f * 16 + i] = near[:, None] * sb[None, :, i]
            tz2[32 + f * 16 + i] = near[None, :] * sb[:, None, i]
        for i in range(CELLS + 2):
            tz2[64 + f * 16 + i] = near[:, None] * sl[None, :, i]
            tz2[96 + f * 16 + i] = near[None, :] * sl[:, None, i]
    t["tz2"] = pair(tz2.reshape(128, 1024))
    return t


def split(x):
    high = x.astype(BF16)
    return high, (x - high.astype(F32)).astype(BF16)


def dot(x, y):
    return lax.dot_general(x, y, (((1,), (0,)), ((), ())), preferred_element_type=F32)


def dot_nt(x, y):
    return lax.dot_general(x, y, (((1,), (1,)), ((), ())), preferred_element_type=F32)


def times_table(x, table):
    high, low = split(x)
    return dot(high, table[0]) + dot(low, table[0]) + dot(high, table[1])


def table_times(table, x, product=dot):
    high, low = split(x)
    return product(table[0], high) + product(table[1], high) + product(table[0], low)


def stacked(x, width):
    return jnp.concatenate([x[:, i : i + width] for i in range(0, x.shape[1], width)], axis=0)


def unstacked(x, rows):
    return jnp.concatenate([x[i : i + rows] for i in range(0, x.shape[0], rows)], axis=1)


def lanes(rows):
    return lax.broadcasted_iota(jnp.int32, (rows, 128), 1)


A_TABLES = ("sc", "bd", "rm", "ty", "tz", "tx1", "tx2", "tx3", "u", "k1", "kl", "wc", "tf", "tc", "ec", "ef")


def first_kernel(q_ref, *refs):
    t = dict(zip(A_TABLES, refs))
    refs = refs[len(A_TABLES) :]
    tb_hbm, ta_hbm, m_ref, own_ref, down_ref, up_ref, rows, ls, lp, ly, g, tb, ta, sem = refs
    a, b = lax.axis_index("gx"), lax.axis_index("gy")
    copy_a = pltpu.make_async_copy(ta_hbm.at[a], ta, sem.at[0])
    copy_b = pltpu.make_async_copy(tb_hbm.at[b], tb, sem.at[1])
    copy_a.start()
    copy_b.start()
    x = table_times(t["sc"], q_ref[...])
    for y in range(P_SIZE):
        rows[pl.ds(y, 64, stride=P_SIZE), :] = x[:, y * 32 : y * 32 + 32]
    x = table_times(t["sc"], rows[...], dot_nt)
    x = times_table(stacked(x, 128), t["bd"]) * t["rm"][...]
    x = times_table(x, t["ty"])
    for i in range(4):
        z = table_times(t["tz"], x[i * 256 : i * 256 + 256])
        for j in range(4):
            k = i * 4 + j
            ls[:, k * 64 : k * 64 + 64] = z[j * 32 : j * 32 + 16, 0:64]
            lp[:, k * 64 : k * 64 + 64] = z[j * 32 + 16 : j * 32 + 32, 64:128]
            ly[:, k * 16 : k * 16 + 16] = z[j * 32 + 16 : j * 32 + 32, 128:144]
    samples = times_table(ls[...], t["tx1"])
    coefs = times_table(lp[...], t["tx2"]) + times_table(ly[...], t["tx3"])
    x = table_times(t["u"], samples)
    coefs = coefs - times_table(x[16:32], t["kl"])
    own_ref[...] = coefs
    down_ref[...] = pltpu.roll(coefs, 128 - 48, 1)
    up_ref[...] = pltpu.roll(coefs, 128 - 80, 1)
    x = times_table(x[0:8], t["k1"]) + x[8:16]
    for i in range(16):
        g[i * 8 : i * 8 + 8, :] = x[:, i * 16 : i * 16 + 16]
    copy_b.wait()
    x = times_table(g[...], tb)
    row = lax.broadcasted_iota(jnp.int32, (128, 512), 0)
    lane = lax.broadcasted_iota(jnp.int32, (128, 512), 1)
    x = jnp.where(row % 8 == lane // 64, x, 0.0)
    copy_a.wait()
    x = table_times(ta, x) * t["wc"][...]
    y_faces = table_times(t["ec"], times_table(x, t["tf"]))
    x_faces = times_table(stacked(table_times(t["ef"], x), 256), t["tc"])
    lane = lanes(N_GX)
    for f in range(2):
        for i in range(N_GY):
            col = i // 2 * 128
            low = x_faces[f * 32 : f * 32 + 32, col : col + 128]
            high = x_faces[64 + f * 32 : 96 + f * 32, col : col + 128]
            if i % 2:
                low = pltpu.roll(low, 64, 1)
            else:
                high = pltpu.roll(high, 64, 1)
            m_ref[pl.ds(i * 4 + f, N_GX, stride=32), :] = jnp.where(lane < 64, low, high)
    turned = [y_faces[i * 32 : i * 32 + 32] for i in range(CELLS + 2)]
    turned = [v if i == 0 else pltpu.roll(v, 8 * i, 1) for i, v in enumerate(turned)]
    group = lane // 8
    for i in range(N_GY):
        for f in range(2):
            value = jnp.zeros((N_GX, 128), F32)
            for k in range(CELLS + 2):
                value = jnp.where(group == (2 * i + f + k) % 16, turned[k], value)
            m_ref[pl.ds(i * 4 + 2 + f, N_GX, stride=32), :] = value


def charge_kernel(q_ref, s_ref, bd_ref, out_ref, rows):
    x = table_times(s_ref, q_ref[...])
    for y in range(P_SIZE):
        rows[pl.ds(y, 32, stride=P_SIZE), :] = x[:, y * 32 : y * 32 + 32]
    x = table_times(s_ref, rows[...], dot_nt)
    out_ref[...] = times_table(stacked(x, 128), bd_ref)


def last_kernel(m_ref, own_ref, right_ref, left_ref, above_ref, below_ref, spec_ref, s_ref, bd_ref, rm_ref,
                sbz_ref, lz_ref, tz_ref, sel_hbm, out_ref, rows, flat, sel, sem):
    copy = pltpu.make_async_copy(sel_hbm.at[lax.axis_index("gy")], sel, sem)
    copy.start()
    got = jnp.sum(m_ref[...].reshape(128, 8, 128), axis=0)
    got = got[0:4] + got[4:8]
    lane = lanes(NL)
    coefs = jnp.where(lane < 64, own_ref[...], 0.0)
    for i, ref in enumerate((left_ref, right_ref, below_ref, above_ref)):
        coefs = coefs + jnp.where(lane // 16 == i, ref[...], 0.0)
    copy.wait()
    high, low = split(jnp.concatenate([lz_ref[i // 2] * got[i : i + 1] for i in range(4)], axis=1))
    x = dot(high, sel[...]) + dot(low, sel[...]) + table_times(sbz_ref, coefs)
    x = times_table(x, tz_ref)
    x = (stacked(x, 128) + spec_ref[...]) * rm_ref[...]
    x = table_times(s_ref, unstacked(x, 32))
    x = times_table(stacked(x, 128), bd_ref)
    for i in range(8):
        rows[i * 128 : i * 128 + 128, :] = x[i * 32 : i * 32 + 32].T
    for y in range(P_SIZE):
        flat[:, y * 32 : y * 32 + 32] = rows[pl.ds(y, 32, stride=P_SIZE), :]
    out_ref[...] = table_times(s_ref, flat[...])


def vmem(count):
    return [pl.BlockSpec(memory_space=pltpu.VMEM)] * count


def hbm(count):
    return [pl.BlockSpec(memory_space=pl.ANY)] * count


def shape(*dims):
    return jax.ShapeDtypeStruct(dims, F32)


PARAMS = pltpu.CompilerParams(vmem_limit_bytes=VMEM_LIMIT)


def body(charge):
    t = {k: jnp.asarray(v) for k, v in tables().items()}
    message, own, down, up = pl.pallas_call(
        first_kernel,
        out_shape=(shape(1024, 128), shape(NL, 128), shape(NL, 128), shape(NL, 128)),
        in_specs=vmem(1 + len(A_TABLES)) + hbm(2),
        out_specs=tuple(vmem(4)),
        scratch_shapes=[
            pltpu.VMEM((2048, 32), F32),
            pltpu.VMEM((16, 1024), F32),
            pltpu.VMEM((16, 1024), F32),
            pltpu.VMEM((16, 256), F32),
            pltpu.VMEM((128, 16), F32),
            pltpu.VMEM((2, 16, 512), BF16),
            pltpu.VMEM((2, 256, 128), BF16),
            pltpu.SemaphoreType.DMA((2,)),
        ],
        compiler_params=PARAMS,
        name="first",
    )(charge, *[t[k] for k in A_TABLES], t["tb"], t["ta"])
    arrived = lax.all_to_all(message.reshape(256, 4, 128), ("gx", "gy"), 0, 0).reshape(1024, 128)
    around = []
    for axis, count in (("gx", N_GX), ("gy", N_GY)):
        forward = [(i, i + 1) for i in range(count - 1)]
        around.append(lax.ppermute(down, axis, [(j, i) for i, j in forward]))
        around.append(lax.ppermute(up, axis, forward))
    spec = pl.pallas_call(
        charge_kernel,
        out_shape=shape(256, 128),
        in_specs=vmem(3),
        out_specs=vmem(1)[0],
        scratch_shapes=[pltpu.VMEM((1024, 32), F32)],
        compiler_params=PARAMS,
        name="charge",
    )(charge, t["s32"], t["bd32"])
    return pl.pallas_call(
        last_kernel,
        out_shape=shape(32, 1024),
        in_specs=vmem(13) + hbm(1),
        out_specs=vmem(1)[0],
        scratch_shapes=[
            pltpu.VMEM((1024, 32), F32),
            pltpu.VMEM((32, 1024), F32),
            pltpu.VMEM((512, 128), BF16),
            pltpu.SemaphoreType.DMA,
        ],
        compiler_params=PARAMS,
        name="last",
    )(arrived, own, *around, spec, t["s32"], t["bd32"], t["rm32"], t["sbz"], t["lz"], t["tz2"], t["sel"])


def solution(mesh):
    spec = P("gx", "gy")
    return jax.shard_map(body, mesh=mesh, in_specs=(spec,), out_specs=spec, check_vma=False)
```

profile of v0, /device:TPU:1, one launch (start us, length us, event | category | flops | bytes accessed | tf_op | source)
XLA Modules:
  0.0 51.3 jit_solution(977063291083934532)
XLA Ops:
  0.0 10.2 %first.1 = (f32[1024,128]{1,0:T(8,128)}, f32[16,128]{1,0:T(8,128)}, f32[16,128]{1,0:T(8,128)}, f32[16,128]{1,0:T(8,128)}) custom-call(f32[32,1024]{1,0:T(8,128)} %q_ref.3, bf16[2,64,32]{2,1,0:T(8,128)(2,1)} %constant.50.clone.refs_0_, bf16[2,128,256]{2,1,0:T(8,128)(2,1)} %constant.51.clone.refs_1_, f32[1024,256]{1,0:T(8,128)} %constant.52.clone.refs_2_, ...), custom_call_target="tpu_custom_call" | custom-call | tf_op jit(solution)/shard_map/first/pallas_call | solution.py:341
  10.2 15.7 %all-to-all-start = ((f32[256,4,128]{2,1,0:T(4,128)}), f32[256,4,128]{2,1,0:T(4,128)S(1)}, u32[]{:S(2)}, u32[]{:S(2)}) async-start(f32[256,4,128]{2,1,0:T(4,128)} %bitcast.3), calls=%async_computation | async-start | bytes 1048576 | tf_op jit(solution)/shard_map/all_to_all | solution.py:359
  25.9 4.1 %collective-permute-start = (f32[16,128]{1,0:T(8,128)}, f32[16,128]{1,0:T(8,128)S(1)}, u32[]{:S(2)}, u32[]{:S(2)}) collective-permute-start(f32[16,128]{1,0:T(8,128)} %get-tuple-element.11), channel_id=1, source_target_pairs={{8,0},{16,8},{24,16},{32,24},{40,32},{48,40},{56,48},{64,56},{72,6... | collective-permute-start | bytes 24584 | tf_op jit(solution)/shard_map/ppermute | solution.py:363
  30.0 1.9 %collective-permute-start.1 = (f32[16,128]{1,0:T(8,128)}, f32[16,128]{1,0:T(8,128)S(1)}, u32[]{:S(2)}, u32[]{:S(2)}) collective-permute-start(f32[16,128]{1,0:T(8,128)} %get-tuple-element.12), channel_id=1, source_target_pairs={{0,8},{8,16},{16,24},{24,32},{32,40},{40,48},{48,56},{56,64},{64,7... | collective-permute-start | bytes 24584 | tf_op jit(solution)/shard_map/ppermute | solution.py:364
  31.9 1.3 %collective-permute-start.2 = (f32[16,128]{1,0:T(8,128)}, f32[16,128]{1,0:T(8,128)S(1)}, u32[]{:S(2)}, u32[]{:S(2)}) collective-permute-start(f32[16,128]{1,0:T(8,128)} %get-tuple-element.11), channel_id=1, source_target_pairs={{1,0},{2,1},{3,2},{4,3},{5,4},{6,5},{7,6},{9,8},{10,9},{11,10},{12... | collective-permute-start | bytes 24584 | tf_op jit(solution)/shard_map/ppermute | solution.py:363
  33.2 4.0 %collective-permute-start.3 = (f32[16,128]{1,0:T(8,128)}, f32[16,128]{1,0:T(8,128)S(1)}, u32[]{:S(2)}, u32[]{:S(2)}) collective-permute-start(f32[16,128]{1,0:T(8,128)} %get-tuple-element.12), channel_id=1, source_target_pairs={{0,1},{1,2},{2,3},{3,4},{4,5},{5,6},{6,7},{8,9},{9,10},{10,11},{11... | collective-permute-start | bytes 24584 | tf_op jit(solution)/shard_map/ppermute | solution.py:364
  37.2 2.6 %charge.1.spec_ref = f32[256,128]{1,0:T(8,128)} custom-call(f32[32,1024]{1,0:T(8,128)} %q_ref.3, bf16[2,32,32]{2,1,0:T(8,128)(2,1)} %constant.68.clone.s_ref, bf16[2,128,128]{2,1,0:T(8,128)(2,1)} %constant.69.clone.bd_ref), custom_call_target="tpu_custom_call" | custom-call | tf_op jit(solution)/shard_map/charge/pallas_call | solution.py:365
  39.7 0.0 collective-permute-done.right_ref
  39.7 0.0 copy-start.1
  39.7 0.0 collective-permute-done.1.left_ref
  39.7 0.0 copy-start.2
  39.8 0.0 collective-permute-done.2.above_ref
  39.8 0.0 copy-start.3
  39.8 0.0 collective-permute-done.3.below_ref
  39.8 0.0 copy-start.4
  39.8 6.2 %all-to-all-done = f32[256,4,128]{2,1,0:T(4,128)S(1)} async-done(((f32[256,4,128]{2,1,0:T(4,128)}), f32[256,4,128]{2,1,0:T(4,128)S(1)}, u32[]{:S(2)}, u32[]{:S(2)}) %all-to-all-start) | async-done | bytes 524320 | tf_op jit(solution)/shard_map/all_to_all | solution.py:359
  46.0 0.0 copy-start
  46.0 0.0 copy-done.1
  46.0 0.0 copy-done.2
  46.0 0.0 copy-done.3
  46.0 0.0 copy-done.4
  46.0 0.8 %copy-done = f32[256,4,128]{2,1,0:T(4,128)} copy-done((f32[256,4,128]{2,1,0:T(4,128)}, f32[256,4,128]{2,1,0:T(4,128)S(1)}, u32[]{:S(2)}) %copy-start) | copy-done | bytes 524312
  46.8 4.5 %last.1 = f32[32,1024]{1,0:T(8,128)} custom-call(f32[1024,128]{1,0:T(8,128)} %bitcast.2, f32[16,128]{1,0:T(8,128)} %get-tuple-element.10.own_ref, f32[16,128]{1,0:T(8,128)} %copy-done.1, f32[16,128]{1,0:T(8,128)} %copy-done.2, f32[16,128]{1,0:T(8,128)} %copy-done.3, f32[16,128]{1,0:T(8,128)} %copy-done.4, f32[256,128]{1,0:T(8,128)} %charge.1.spec_ref, ...), custom_call_target="tpu_custom_call" | custom-call | tf_op jit(solution)/shard_map/last/pallas_call | solution.py:374
Async XLA Ops:
  10.2 35.8 %all-to-all-start = ((f32[256,4,128]{2,1,0:T(4,128)}), f32[256,4,128]{2,1,0:T(4,128)S(1)}, u32[]{:S(2)}, u32[]{:S(2)}) async-start(f32[256,4,128]{2,1,0:T(4,128)} %bitcast.3), calls=%async_computation | async-start | bytes 1048576 | tf_op jit(solution)/shard_map/all_to_all | solution.py:359
  25.9 13.8 %collective-permute-start = (f32[16,128]{1,0:T(8,128)}, f32[16,128]{1,0:T(8,128)S(1)}, u32[]{:S(2)}, u32[]{:S(2)}) collective-permute-start(f32[16,128]{1,0:T(8,128)} %get-tuple-element.11), channel_id=1, source_target_pairs={{8,0},{16,8},{24,16},{32,24},{40,32},{48,40},{56,48},{64,56},{72,6... | collective-permute-start | bytes 24584 | tf_op jit(solution)/shard_map/ppermute | solution.py:363
  30.0 9.8 %collective-permute-start.1 = (f32[16,128]{1,0:T(8,128)}, f32[16,128]{1,0:T(8,128)S(1)}, u32[]{:S(2)}, u32[]{:S(2)}) collective-permute-start(f32[16,128]{1,0:T(8,128)} %get-tuple-element.12), channel_id=1, source_target_pairs={{0,8},{8,16},{16,24},{24,32},{32,40},{40,48},{48,56},{56,64},{64,7... | collective-permute-start | bytes 24584 | tf_op jit(solution)/shard_map/ppermute | solution.py:364
  31.9 7.9 %collective-permute-start.2 = (f32[16,128]{1,0:T(8,128)}, f32[16,128]{1,0:T(8,128)S(1)}, u32[]{:S(2)}, u32[]{:S(2)}) collective-permute-start(f32[16,128]{1,0:T(8,128)} %get-tuple-element.11), channel_id=1, source_target_pairs={{1,0},{2,1},{3,2},{4,3},{5,4},{6,5},{7,6},{9,8},{10,9},{11,10},{12... | collective-permute-start | bytes 24584 | tf_op jit(solution)/shard_map/ppermute | solution.py:363
  33.2 6.6 %collective-permute-start.3 = (f32[16,128]{1,0:T(8,128)}, f32[16,128]{1,0:T(8,128)S(1)}, u32[]{:S(2)}, u32[]{:S(2)}) collective-permute-start(f32[16,128]{1,0:T(8,128)} %get-tuple-element.12), channel_id=1, source_target_pairs={{0,1},{1,2},{2,3},{3,4},{4,5},{5,6},{6,7},{8,9},{9,10},{10,11},{11... | collective-permute-start | bytes 24584 | tf_op jit(solution)/shard_map/ppermute | solution.py:364
  39.7 6.3 %copy-start.1 = (f32[16,128]{1,0:T(8,128)}, f32[16,128]{1,0:T(8,128)S(1)}, u32[]{:S(2)}) copy-start(f32[16,128]{1,0:T(8,128)S(1)} %collective-permute-done.right_ref) | copy-start | bytes 24580
  39.7 6.3 %copy-start.2 = (f32[16,128]{1,0:T(8,128)}, f32[16,128]{1,0:T(8,128)S(1)}, u32[]{:S(2)}) copy-start(f32[16,128]{1,0:T(8,128)S(1)} %collective-permute-done.1.left_ref) | copy-start | bytes 24580
  39.8 6.3 %copy-start.3 = (f32[16,128]{1,0:T(8,128)}, f32[16,128]{1,0:T(8,128)S(1)}, u32[]{:S(2)}) copy-start(f32[16,128]{1,0:T(8,128)S(1)} %collective-permute-done.2.above_ref) | copy-start | bytes 24580
  39.8 6.2 %copy-start.4 = (f32[16,128]{1,0:T(8,128)}, f32[16,128]{1,0:T(8,128)S(1)}, u32[]{:S(2)}) copy-start(f32[16,128]{1,0:T(8,128)S(1)} %collective-permute-done.3.below_ref) | copy-start | bytes 24580
  46.0 0.8 %copy-start = (f32[256,4,128]{2,1,0:T(4,128)}, f32[256,4,128]{2,1,0:T(4,128)S(1)}, u32[]{:S(2)}) copy-start(f32[256,4,128]{2,1,0:T(4,128)S(1)} %all-to-all-done) | copy-start | bytes 1572868
where the time goes:
time: 51.6 us; the launch traced here: 51.3 us
  starting transfers between devices  26.9 us (52%)
  Pallas kernels  17.2 us (33%)
  waiting for transfers between devices  6.22 us (12%)
  local copies, waits for them, and re-layouts  0.78 us (2%)
    all_to_all x1, starting transfers between devices, body(): lax.all_to_all(message.reshape(256, 4, 128), ('gx', 'gy'), 0, 0)  15.7 us
    pallas_call x1, Pallas kernels, body(): pl.pallas_call(first_kernel, out_shape=(shape(1024, 128), shape(NL, 128),...  10.2 us
    all_to_all x1, waiting for transfers between devices, body(): lax.all_to_all(message.reshape(256, 4, 128), ('gx', 'gy'), 0, 0)  6.21 us
    ppermute x2, starting transfers between devices, body(): around.append(lax.ppermute(up, axis, forward))  5.91 us
    ppermute x2, starting transfers between devices, body(): around.append(lax.ppermute(down, axis, [(j, i) for i, j in forward]))  5.35 us
    pallas_call x1, Pallas kernels, body(): pl.pallas_call(last_kernel, out_shape=shape(32, 1024), in_specs=vmem(13)...  4.46 us
    pallas_call x1, Pallas kernels, body(): pl.pallas_call(charge_kernel, out_shape=shape(256, 128), in_specs=vmem(3)...  2.56 us
  transfers between devices with their start and end apart: 5, of which 1 were waited for; matrix products, arithmetic and copies ran while one was open for 0% of the time, Pallas kernels for 5%

commit v1 on v0

v1 whole, which is shorter than its diff:
```python
import functools

import jax
import jax.numpy as jnp
import ml_dtypes
import numpy as np
from jax import lax
from jax.experimental import pallas as pl
from jax.experimental.pallas import tpu as pltpu
from jax.sharding import PartitionSpec as P

P_SIZE = 32
W = 16
Q = 4
NL = 16
N_GX = 32
N_GY = 8
CELLS = P_SIZE // Q
BF16 = jnp.bfloat16
F32 = jnp.float32


def sine(length):
    counter = np.arange(length) + 1
    multiple = counter[:, None] * counter[None, :] % (2 * (length + 1))
    return np.sin(np.pi * multiple / (length + 1))


def eigen(length):
    return 2.0 - 2.0 * np.cos(np.pi * (np.arange(length) + 1) / (length + 1))


def interp(fine_start, fine_count, coarse_start, coarse_count, ratio):
    fine_pos = np.arange(fine_count) + fine_start
    coarse_pos = np.arange(coarse_count) + coarse_start
    numerator = 2 * fine_pos - (ratio - 1)
    lower_index = numerator // (2 * ratio)
    weight = ((numerator - 2 * ratio * lower_index) / (2.0 * ratio))[:, None]
    below = (coarse_pos[None, :] == lower_index[:, None]).astype(np.float64)
    above = (coarse_pos[None, :] == lower_index[:, None] + 1).astype(np.float64)
    return below * (1.0 - weight) + above * weight


def legendre(length, count):
    points = (2.0 * np.arange(length) + 1.0) / length - 1.0
    columns = [np.ones_like(points), points]
    for degree in range(2, count):
        columns.append(
            ((2 * degree - 1) * points * columns[-1] - (degree - 1) * columns[-2]) / degree
        )
    result = []
    for column in columns[:count]:
        vector = column
        for _ in range(2):
            for earlier in result:
                vector = vector - np.sum(earlier * vector) * earlier
        result.append(vector / np.sqrt(np.sum(vector * vector)))
    return np.stack(result, axis=1)


def columns_at(table, positions):
    positions = np.asarray(positions)
    inside = (positions >= 0) & (positions < table.shape[1])
    return table[:, np.clip(positions, 0, table.shape[1] - 1)] * inside


def pair(table):
    table = np.asarray(table, np.float64)
    high = table.astype(np.float32).astype(ml_dtypes.bfloat16)
    low = (table - high.astype(np.float64)).astype(np.float32).astype(ml_dtypes.bfloat16)
    return np.stack([high, low], axis=-3)


@functools.lru_cache(None)
def tables():
    t = {}
    n = P_SIZE + 2 * W
    s64, m64 = sine(n), eigen(n)
    s32, m32 = sine(P_SIZE), eigen(P_SIZE)
    s8, m8 = sine(CELLS), eigen(CELLS)
    nx, ny = CELLS * N_GX, CELLS * N_GY
    sx, mx = sine(nx), eigen(nx)
    sy, my = sine(ny), eigen(ny)
    eye = np.eye
    basis = legendre(P_SIZE, NL)
    fine = interp(0, n, 0, n // Q, Q)
    mean = np.kron(eye(n // Q), np.full((1, Q), 1.0 / Q))
    inside = slice(W, W + P_SIZE)
    places = [W - 1, W + P_SIZE, W, W + P_SIZE - 1]
    r = mean @ s64
    bs = basis.T @ s64[inside]
    st = s64[places]
    bl = basis.T @ fine[inside]
    lt = fine[places]
    lanes_x, lanes_y = [[0], [16], [128, 144], [160, 176]], [[32], [48], [192, 208], [224, 240]]
    sc = s64[:, inside]
    t["sc"] = pair(sc)
    t["bd"] = pair(np.kron(eye(4), sc.T))
    kx = m64.reshape(16, 1, 4, 1)
    rm = (2.0 / (n + 1)) ** 3 / (kx + m64.reshape(1, n, 1, 1) + m64.reshape(1, 1, 1, n))
    t["rm"] = rm.reshape(16 * n, 4 * n).astype(np.float32)
    ty = np.zeros((4, n, 256))
    for i in range(4):
        ty[i, :, i * 16 : i * 16 + 16] = r.T
        ty[i, :, 64 + i * 16 : 64 + i * 16 + 16] = bs.T
        ty[i, :, 128 + i * 4 : 128 + i * 4 + 4] = st.T
    t["ty"] = pair(ty.reshape(4 * n, 256))
    t["tz"] = pair(np.kron(eye(4), np.concatenate([r, bs], axis=0)))
    t["tx1"] = pair(np.kron(r.T, eye(16)))
    tx2 = np.zeros((n, NL, 256))
    tx3 = np.zeros((n, 4, 256))
    kl = np.zeros((16, 16, 256))
    for i in range(4):
        for lane in lanes_x[i]:
            tx2[:, :, lane : lane + NL] = st[i][:, None, None] * eye(NL)
            kl[:, :, lane : lane + NL] = lt[i][:, None, None] * bl.T[None]
        for lane in lanes_y[i]:
            tx3[:, i, lane : lane + NL] = bs.T
            kl[:, :, lane : lane + NL] = bl.T[:, None, :] * lt[i][None, :, None]
    t["tx2"] = pair(tx2.reshape(n * NL, 256))
    t["tx3"] = pair(tx3.reshape(n * 4, 256))
    t["kl"] = pair(kl.reshape(256, 256))
    first = W // Q
    u1 = np.zeros((CELLS, 16))
    u2 = np.zeros((CELLS, 16))
    for k in range(CELLS):
        u1[:, k + first] += s8[:, k]
        u2[:, k + first - 1] -= s8[:, k] / (Q * Q)
        u2[:, k + first + 1] -= s8[:, k] / (Q * Q)
    t["u"] = pair(np.concatenate([u1, u2, bl], axis=0))
    beside = eye(16, k=1) + eye(16, k=-1)
    k1 = 6.0 * eye(256) - np.kron(beside, eye(16)) - np.kron(eye(16), beside)
    t["k1"] = pair(k1 / (Q * Q))
    t["yb"] = pair(np.concatenate([columns_at(sy, np.arange(16) + b * CELLS - first) for b in range(N_GY)], axis=1))
    xa = [columns_at(sx, np.arange(16) + a * CELLS - first) for a in range(N_GX)]
    xa = [np.concatenate(xa[2 * i : 2 * i + 2], axis=1).T for i in range(N_GX // 2)]
    t["xa"] = pair(np.stack([np.repeat(v, CELLS, axis=0) for v in xa]))
    scale = Q * Q * (2.0 / (nx + 1)) * (2.0 / (ny + 1)) * (2.0 / (CELLS + 1))
    wc = scale / (m8.reshape(CELLS, 1, 1) + my.reshape(1, ny, 1) + mx.reshape(1, 1, nx))
    t["wc"] = wc.reshape(CELLS * ny, nx).astype(np.float32)
    edge = interp(-1, P_SIZE + 2, -1, CELLS + 2, Q)
    ends = edge[[0, P_SIZE + 1]]
    lateral = edge[1 : P_SIZE + 1]
    depth = interp(0, P_SIZE, 0, CELLS, Q)
    around = np.arange(CELLS + 2) - 1
    near = [columns_at(sy, around + b * CELLS).T for b in range(N_GY)]
    near = [np.concatenate([v, ends @ v, np.zeros((4, ny))], axis=0) for v in near]
    ey = np.zeros((N_GY, 16, CELLS, CELLS, ny))
    for k in range(CELLS):
        ey[:, :, k, k, :] = np.stack(near)
    t["ey"] = pair(ey.reshape(N_GY, 128, CELLS * ny))
    near = [columns_at(sx, around + a * CELLS).T for a in range(N_GX)]
    near = np.stack([np.concatenate([v, ends @ v], axis=0) for v in near]).reshape(N_GX // 2, 2, 12, nx)
    t["ex"] = pair(near.transpose(1, 2, 0, 3).reshape(2, 12 * (N_GX // 2), nx))
    t["s32"] = pair(s32)
    t["bd32"] = pair(np.kron(eye(4), s32))
    rm32 = m32.reshape(8, 1, 4, 1) + m32.reshape(1, 32, 1, 1) + m32.reshape(1, 1, 1, 32)
    t["rm32"] = ((2.0 / (P_SIZE + 1)) ** 3 / rm32).reshape(256, 128).astype(np.float32)
    t["sbz"] = pair(s32 @ basis)
    lz = s32 @ depth @ s8
    lane = np.arange(128)
    t["lz"] = lz[:, lane % 8].astype(np.float32)
    sel = np.zeros((4, 128, 128), np.float32)
    for f in range(4):
        for i in range((CELLS + 2) * CELLS):
            sel[f, i, 64 + f * 16 + i // 8] = 1.0
    t["sel"] = sel.reshape(512, 128).astype(ml_dtypes.bfloat16)
    tz2 = np.zeros((128, 32, 32))
    sb, sl = s32 @ basis, s32 @ lateral
    for f, layer in enumerate([0, P_SIZE - 1]):
        near = s32[:, layer]
        for i in range(NL):
            tz2[f * 16 + i] = near[:, None] * sb[None, :, i]
            tz2[32 + f * 16 + i] = near[None, :] * sb[:, None, i]
        for i in range(CELLS + 2):
            tz2[64 + f * 16 + i] = near[:, None] * sl[None, :, i]
            tz2[96 + f * 16 + i] = near[None, :] * sl[:, None, i]
    t["tz2"] = pair(tz2.reshape(128, 1024))
    return t


def split(x):
    high = x.astype(BF16)
    return high, (x - high.astype(F32)).astype(BF16)


def dot(x, y):
    return lax.dot_general(x, y, (((1,), (0,)), ((), ())), preferred_element_type=F32)


def dot_nt(x, y):
    return lax.dot_general(x, y, (((1,), (1,)), ((), ())), preferred_element_type=F32)


def times_table(x, table):
    high, low = split(x)
    return dot(high, table[0]) + dot(low, table[0]) + dot(high, table[1])


def table_times(table, x, product=dot):
    high, low = split(x)
    return product(table[0], high) + product(table[1], high) + product(table[0], low)


def stacked(x, width):
    return jnp.concatenate([x[:, i : i + width] for i in range(0, x.shape[1], width)], axis=0)


def unstacked(x, rows):
    return jnp.concatenate([x[i : i + rows] for i in range(0, x.shape[0], rows)], axis=1)


def lanes(rows):
    return lax.broadcasted_iota(jnp.int32, (rows, 128), 1)


class Loaded:
    def __init__(self, names, sources, targets, sem):
        self.refs = dict(zip(names, targets))
        self.copies = {
            name: pltpu.make_async_copy(source, target, sem.at[i])
            for i, (name, source, target) in enumerate(zip(names, sources, targets))
        }
        for name in names:
            self.copies[name].start()

    def __getitem__(self, name):
        if name in self.copies:
            self.copies.pop(name).wait()
        return self.refs[name]


def kind(name):
    table = tables()[name]
    dims = table.shape[1:] if name in ("xa", "ey", "ex") else table.shape
    return dims, F32 if table.dtype == np.float32 else BF16


A_TABLES = ("sc", "bd", "rm", "ty", "tz", "tx1", "u", "k1", "tx2", "tx3", "kl", "s32", "bd32")
B_TABLES = ("yb", "xa", "wc", "ey", "ex")
C_TABLES = ("lz", "sel", "sbz", "tz2", "rm32", "s32", "bd32")
LATER = B_TABLES + C_TABLES


def first_kernel(q_ref, *refs):
    n, later = len(A_TABLES), len(LATER)
    own_tables, later_tables, refs = refs[:n], refs[n : n + later], refs[n + later :]
    m_ref, own_ref, spec_ref = refs[:3]
    fetched, refs = refs[3 : 3 + later], refs[3 + later :]
    rows, rows32, ls, lp, ly, spill = refs[:6]
    t = Loaded(A_TABLES, own_tables, refs[6 : 6 + n], refs[6 + n])
    place = {"xa": lax.axis_index("gs"), "ey": lax.axis_index("gy"), "ex": lax.axis_index("gc")}
    sources = [ref.at[place[k]] if k in place else ref for k, ref in zip(LATER, later_tables)]
    ahead = Loaded(LATER, sources, fetched, refs[7 + n])
    x = table_times(t["sc"], q_ref[...])
    for y in range(P_SIZE):
        rows[pl.ds(y, 64, stride=P_SIZE), :] = x[:, y * 32 : y * 32 + 32]
    x = table_times(t["sc"], rows[...], dot_nt)
    x = times_table(stacked(x, 128), t["bd"]) * t["rm"][...]
    x = times_table(x, t["ty"])
    for i in range(4):
        z = table_times(t["tz"], x[i * 256 : i * 256 + 256])
        for j in range(4):
            k = i * 4 + j
            ls[:, k * 64 : k * 64 + 64] = z[j * 32 : j * 32 + 16, 0:64]
            lp[:, k * 64 : k * 64 + 64] = z[j * 32 + 16 : j * 32 + 32, 64:128]
            ly[:, k * 16 : k * 16 + 16] = z[j * 32 + 16 : j * 32 + 32, 128:144]
    samples = times_table(ls[...], t["tx1"])
    coefs = times_table(lp[...], t["tx2"]) + times_table(ly[...], t["tx3"])
    x = table_times(t["u"], samples)
    coefs = coefs - times_table(x[16:32], t["kl"])
    own_ref[...] = coefs[:, 0:128]
    y = table_times(t["s32"], q_ref[...])
    for i in range(P_SIZE):
        rows32[pl.ds(i, 32, stride=P_SIZE), :] = y[:, i * 32 : i * 32 + 32]
    y = table_times(t["s32"], rows32[...], dot_nt)
    spec_ref[...] = times_table(stacked(y, 128), t["bd32"])
    x = (times_table(x[0:8], t["k1"]) + x[8:16]).T
    for i in range(16):
        spill[:, i * 8 : i * 8 + 8] = x[i * 16 : i * 16 + 16]
    spilled = spill[...]
    tile = jnp.where(lanes(8) // 16 % 2 == 0, coefs[0:8, 128:256], coefs[8:16, 128:256])
    for i in range(16):
        m_ref[i * 24 : i * 24 + 16, :] = spilled
        m_ref[i * 24 + 16 : i * 24 + 24, :] = tile
    for name in LATER:
        ahead[name]


def unpacked(tile, source, slot):
    parts = []
    for half in range(2):
        shift = (16 * slot - source - 16 * half) % 128
        parts.append(pltpu.roll(tile, shift, 1) if shift else tile)
    return jnp.where(lanes(NL) // 16 == slot, jnp.concatenate(parts, axis=0), 0.0)


def strip_kernel(got_ref, own_ref, *refs):
    t = dict(zip(B_TABLES, refs))
    m_ref, coefs_ref = refs[len(B_TABLES) :]
    s, c, b = lax.axis_index("gs"), lax.axis_index("gc"), lax.axis_index("gy")
    source = [
        jnp.concatenate([got_ref[(i * 8 + j) * 24 : (i * 8 + j) * 24 + 16, :] for j in range(N_GY)], axis=0)
        for i in range(2)
    ]
    x = table_times(t["yb"], jnp.concatenate(source, axis=1))
    lane = lax.broadcasted_iota(jnp.int32, (64, 256), 1)
    x = jnp.concatenate([jnp.where(lane % 8 == k, x, 0.0) for k in range(CELLS)], axis=0)
    x = times_table(x, t["xa"]) * t["wc"][...]
    x = table_times(t["ey"], x)
    x = table_times(t["ex"], x, dot_nt)
    m_ref[...] = jnp.zeros((128, 128), F32)
    lane = lanes(16)
    for f in range(2):
        m_ref[pl.ds(f, 16, stride=8), :] = jnp.where(lane < 80, x[160 + f * 16 : 176 + f * 16], 0.0)
        value = jnp.zeros((16, 128), F32)
        for k in range(CELLS + 2):
            part = pltpu.roll(x[k * 16 : k * 16 + 16], (8 * (k - 10 - f)) % 128, 1)
            value = jnp.where(lane // 8 == k, part, value)
        m_ref[pl.ds(2 + f, 16, stride=8), :] = value

    def tile_of(i, j):
        return got_ref[pl.ds(pl.multiple_of((i * 8 + j) * 24 + 16, 8), 8), :]

    partner = tile_of(1 - c, b)
    outside = jnp.where(c == 0, pltpu.roll(partner, 64, 1), pltpu.roll(partner, 96, 1))
    outside = jnp.where(lanes(8) >= 96, outside, 0.0)
    target = s + 1 - 2 * c

    @pl.when((target >= 0) & (target < 16))
    def _():
        where = pl.ds(pl.multiple_of(target * 8, 8), 8)
        m_ref[where, :] = m_ref[where, :] + outside

    coefs = jnp.where(lane < 64, own_ref[...], 0.0)
    coefs = coefs + jnp.where(c == 0, unpacked(partner, 0, 1), unpacked(partner, 32, 0))
    above = unpacked(tile_of(c, jnp.minimum(b + 1, N_GY - 1)), 64, 3)
    below = unpacked(tile_of(c, jnp.maximum(b - 1, 0)), 96, 2)
    coefs = coefs + jnp.where(b < N_GY - 1, above, 0.0) + jnp.where(b > 0, below, 0.0)
    coefs_ref[...] = coefs


def last_kernel(m_ref, coefs_ref, spec_ref, *refs):
    t = dict(zip(C_TABLES, refs))
    out_ref, rows, flat = refs[len(C_TABLES) :]
    got = jnp.sum(m_ref[...].reshape(16, 8, 128), axis=0)
    coefs = coefs_ref[...] + jnp.where(lax.axis_index("gc") == 0, unpacked(got, 96, 0), unpacked(got, 96, 1))
    lz = t["lz"][...]
    sel = t["sel"][...]
    high, low = split(jnp.concatenate([lz * got[i : i + 1] for i in range(4)], axis=1))
    x = dot(high, sel) + dot(low, sel) + table_times(t["sbz"], coefs)
    x = times_table(x, t["tz2"])
    x = (stacked(x, 128) + spec_ref[...]) * t["rm32"][...]
    x = table_times(t["s32"], unstacked(x, 32))
    x = times_table(stacked(x, 128), t["bd32"])
    for i in range(8):
        rows[i * 128 : i * 128 + 128, :] = x[i * 32 : i * 32 + 32].T
    for y in range(P_SIZE):
        flat[:, y * 32 : y * 32 + 32] = rows[pl.ds(y, 32, stride=P_SIZE), :]
    out_ref[...] = table_times(t["s32"], flat[...])


def vmem(count):
    return [pl.BlockSpec(memory_space=pltpu.VMEM)] * count


def hbm(count):
    return [pl.BlockSpec(memory_space=pltpu.HBM)] * count


def shape(*dims):
    return jax.ShapeDtypeStruct(dims, F32)


def params(mib):
    return pltpu.CompilerParams(vmem_limit_bytes=mib * 1024 * 1024)


def body(charge):
    t = {k: jnp.asarray(v) for k, v in tables().items()}
    message, own, spec, *fetched = pl.pallas_call(
        first_kernel,
        out_shape=[shape(384, 128), shape(NL, 128), shape(256, 128)] + [jax.ShapeDtypeStruct(*kind(k)) for k in LATER],
        in_specs=vmem(1) + hbm(len(A_TABLES) + len(LATER)),
        out_specs=vmem(3 + len(LATER)),
        scratch_shapes=[
            pltpu.VMEM((2048, 32), F32),
            pltpu.VMEM((1024, 32), F32),
            pltpu.VMEM((16, 1024), F32),
            pltpu.VMEM((16, 1024), F32),
            pltpu.VMEM((16, 256), F32),
            pltpu.VMEM((16, 128), F32),
        ]
        + [pltpu.VMEM(*kind(k)) for k in A_TABLES]
        + [pltpu.SemaphoreType.DMA((len(A_TABLES),)), pltpu.SemaphoreType.DMA((len(LATER),))],
        compiler_params=params(24),
        name="first",
    )(*[pltpu.with_memory_space_constraint(v, pltpu.HBM) for v in (charge, *[t[k] for k in A_TABLES + LATER])])
    fetched = dict(zip(LATER, fetched))
    strip = lax.all_to_all(message.reshape(16, 24, 128), ("gc", "gy"), 0, 0).reshape(384, 128)
    message, coefs = pl.pallas_call(
        strip_kernel,
        out_shape=(shape(128, 128), shape(NL, 128)),
        in_specs=vmem(2 + len(B_TABLES)),
        out_specs=tuple(vmem(2)),
        compiler_params=params(12),
        name="strip",
    )(strip, own, *[fetched[k] for k in B_TABLES])
    arrived = lax.all_to_all(message.reshape(16, 8, 128), "gs", 0, 0).reshape(128, 128)
    return pl.pallas_call(
        last_kernel,
        out_shape=shape(32, 1024),
        in_specs=vmem(3 + len(C_TABLES)),
        out_specs=vmem(1)[0],
        scratch_shapes=[pltpu.VMEM((1024, 32), F32), pltpu.VMEM((32, 1024), F32)],
        compiler_params=params(12),
        name="last",
    )(arrived, coefs, spec, *[fetched[k] for k in C_TABLES])


def solution(mesh):
    strips = jax.sharding.Mesh(mesh.devices.reshape(N_GX // 2, 2, N_GY), ("gs", "gc", "gy"))
    spec = P(("gs", "gc"), "gy")
    return jax.shard_map(body, mesh=strips, in_specs=(spec,), out_specs=spec, check_vma=False)
```

time: 51.6 us -> 45.5 us (0.88)
  blocking collectives: 0 us -> 32.7 us
  starting transfers between devices: 26.9 us -> 0 us
  waiting for transfers between devices: 6.22 us -> 0 us
  Pallas kernels: 17.2 us -> 12.7 us
  local copies, waits for them, and re-layouts: 0.78 us -> 0 us
    all_to_all x0 -> x2, blocking collectives: none -> 32.7 us  [the longest x1 19.4 us: body(): lax.all_to_all(message.reshape(16, 8, 128), 'gs', 0, 0).reshape(128, 128)]
    all_to_all x1 -> x0, starting transfers between devices: 15.7 us -> none  [body(): lax.all_to_all(message.reshape(256, 4, 128), ('gx', 'gy'), 0, 0)]
    ppermute x4 -> x0, starting transfers between devices: 11.3 us -> none  [the longest x2 5.91 us: body(): around.append(lax.ppermute(up, axis, forward))]
    all_to_all x1 -> x0, waiting for transfers between devices: 6.21 us -> none  [body(): lax.all_to_all(message.reshape(256, 4, 128), ('gx', 'gy'), 0, 0)]
    pallas_call x3, Pallas kernels: 17.2 us -> 12.7 us  [the longest x1 9.15 us: body(): pl.pallas_call(first_kernel, out_shape=[shape(384, 128), shape(NL, 128),...]
    unnamed x10 -> x0, local copies, waits for them, and re-layouts: 0.78 us -> none
  transfers between devices with their start and end apart: 5 -> 0, of which waited for: 1 -> 0; matrix products, arithmetic and copies ran while one was open for 0% -> 0% of each run, Pallas kernels for 5% -> 0%
where the time goes in v1:
time: 45.5 us; the launch traced here: 45.4 us
  blocking collectives  32.7 us (72%)
  Pallas kernels  12.7 us (28%)
    all_to_all x1, blocking collectives, body(): lax.all_to_all(message.reshape(16, 8, 128), 'gs', 0, 0).reshape(128, 128)  19.4 us
    all_to_all x1, blocking collectives, body(): lax.all_to_all(message.reshape(16, 24, 128), ('gc', 'gy'), 0, 0)  13.3 us
    pallas_call x1, Pallas kernels, body(): pl.pallas_call(first_kernel, out_shape=[shape(384, 128), shape(NL, 128),...  9.15 us
    pallas_call x1, Pallas kernels, body(): pl.pallas_call(last_kernel, out_shape=shape(32, 1024), in_specs=vmem(3 +...  2.13 us
    pallas_call x1, Pallas kernels, body(): pl.pallas_call(strip_kernel, out_shape=(shape(128, 128), shape(NL, 128)),...  1.4 us

profile of v1, /device:TPU:1, one launch (start us, length us, event | category | flops | bytes accessed | tf_op | source)
XLA Modules:
  0.0 45.4 jit_solution(4382047969045880486)
XLA Ops:
  0.0 9.1 %first.1 = (f32[384,128]{1,0:T(8,128)S(1)}, f32[16,128]{1,0:T(8,128)S(1)}, f32[256,128]{1,0:T(8,128)S(1)}, bf16[2,64,128]{2,1,0:T(8,128)(2,1)S(1)}, bf16[2,256,2...) custom-call(f32[32,1024]{1,0:T(8,128)} %q_ref.1, ...), custom_call_target="tpu_custom_call" | custom-call | tf_op jit(solution)/shard_map/first/pallas_call | solution.py:381
  9.2 13.3 %all_to_all.10 = f32[16,24,128]{2,1,0:T(8,128)S(1)} all-to-all(f32[16,24,128]{2,1,0:T(8,128)S(1)} %bitcast.6), channel_id=1, replica_groups=mesh['gs'=16,'gc'=2,'gy'=8] {'gc','gy'}, dimensions={0} | all-to-all | bytes 393216 | tf_op jit(solution)/shard_map/all_to_all | solution.py:400
  22.4 1.4 %strip.1 = (f32[128,128]{1,0:T(8,128)S(1)}, f32[16,128]{1,0:T(8,128)S(1)}) custom-call(f32[384,128]{1,0:T(8,128)S(1)} %bitcast.4, f32[16,128]{1,0:T(8,128)S(1)} %get-tuple-element.23.own_ref, bf16[2,64,128]{2,1,0:T(8,128)(2,1)S(1)} %get-tuple-element.24.refs_0_, bf16[2,256,256]{2,1,0:T(8,128)(2,1)S(1)} %get-tuple-element.25.refs_1_, ...), custom_call_target="tpu_custom_call" | custom-call | tf_op jit(solution)/shard_map/strip/pallas_call | solution.py:401
  23.8 19.4 %all_to_all.11 = f32[16,8,128]{2,1,0:T(8,128)S(1)} all-to-all(f32[16,8,128]{2,1,0:T(8,128)S(1)} %bitcast.7), channel_id=1, replica_groups=mesh['gs'=16,'gc'=2,'gy'=8] {'gs'}, dimensions={0} | all-to-all | bytes 131072 | tf_op jit(solution)/shard_map/all_to_all | solution.py:409
  43.3 2.1 %last.1 = f32[32,1024]{1,0:T(8,128)} custom-call(f32[128,128]{1,0:T(8,128)S(1)} %bitcast.5, f32[16,128]{1,0:T(8,128)S(1)} %get-tuple-element.30.coefs_ref, f32[256,128]{1,0:T(8,128)S(1)} %get-tuple-element.31.spec_ref, f32[32,128]{1,0:T(8,128)S(1)} %get-tuple-element.32.refs_0_, bf16[512,128]{1,0:T(8,128)(2,1)S(1)} %get-tuple-element.33.refs_1_, ...), custom_call_target="tpu_custom_call" | custom-call | tf_op jit(solution)/shard_map/last/pallas_call | solution.py:410

commit v2 on v1

--- a/solution.py
+++ b/solution.py
@@ -179,6 +179,61 @@
     return t
 
 
+WIDE = {"bd": (0, 128), "ty": (128, 256), "tz": (384, 128), "tx1": (512, 1024), "k1": (1536, 256), "tx2": (1792, 1024), "tx3": (2816, 256), "kl": (3072, 256)}
+SMALL = {"sc|": (0, 0, 64, 0, 96), "s32|": (0, 64, 32, 0, 96), "u|": (0, 96, 32, 0, 48), "sc=": (1, 0, 128, 0, 64), "s32=": (1, 0, 64, 64, 64)}
+
+
+def in_row(table):
+    return np.concatenate([table[0], table[1], table[0]], axis=1)
+
+
+def in_block(table):
+    return np.block([[table[0], table[0]], [table[1], np.zeros_like(table[1])]])
+
+
+@functools.lru_cache(None)
+def packs():
+    t = tables()
+    small = np.zeros((2, 256, 128), ml_dtypes.bfloat16)
+    for name, (which, row, rows, lane, width) in SMALL.items():
+        form = in_row if name[-1] == "|" else in_block
+        small[which, row : row + rows, lane : lane + width] = form(t[name[:-1]])
+    small[:, 128:256] = t["bd32"]
+    later = np.zeros((2, 128, 1408), ml_dtypes.bfloat16)
+    later[:, :, :1024] = t["tz2"]
+    later[:, :64, 1024:1152] = t["yb"]
+    later[0, 64:96, 1024:1072] = in_row(t["sbz"])
+    later[:, :, 1152:] = t["sel"].reshape(2, 2, 128, 128).transpose(0, 2, 1, 3).reshape(2, 128, 256)
+    scales = np.zeros((768, 256), np.float32)
+    scales[:512] = t["wc"]
+    scales[512:, :128] = t["rm32"]
+    scales[512:544, 128:] = t["lz"]
+    return {
+        "small": small,
+        "wide": np.concatenate([t[name] for name in WIDE], axis=1),
+        "rm": t["rm"],
+        "xa": t["xa"],
+        "ey": t["ey"],
+        "ex": t["ex"],
+        "later": later,
+        "scales": scales,
+    }
+
+
+class View:
+    def __init__(self, ref, row, rows, lane, width):
+        self.ref, self.rows, self.lanes = ref, slice(row, row + rows), slice(lane, lane + width)
+        self.shape = (2, rows, width)
+
+    def __getitem__(self, part):
+        return self.ref[slice(None) if part is Ellipsis else part, self.rows, self.lanes]
+
+
+def small_table(ref, name):
+    which, row, rows, lane, width = SMALL[name]
+    return ref[which, row : row + rows, lane : lane + width]
+
+
 def split(x):
     high = x.astype(BF16)
     return high, (x - high.astype(F32)).astype(BF16)
@@ -194,12 +249,40 @@
 
 def times_table(x, table):
     high, low = split(x)
-    return dot(high, table[0]) + dot(low, table[0]) + dot(high, table[1])
+    rows = x.shape[0]
+    if rows > 128:
+        return dot(jnp.concatenate([high, low, high], axis=1), jnp.concatenate([table[0], table[0], table[1]], axis=0))
+    if rows % 16:
+        return dot(high, table[0]) + dot(low, table[0]) + dot(high, table[1])
+    both = dot(jnp.concatenate([high, low], axis=0), table[0])
+    return both[:rows] + both[rows:] + dot(high, table[1])
 
 
 def table_times(table, x, product=dot):
     high, low = split(x)
-    return product(table[0], high) + product(table[1], high) + product(table[0], low)
+    rows = table.shape[1]
+    both = product(table[...].reshape(2 * rows, table.shape[2]), high)
+    return both[:rows] + both[rows:] + product(table[0], low)
+
+
+def row_times(table, x):
+    high, low = split(x)
+    return dot(table, jnp.concatenate([high, high, low], axis=0))
+
+
+def block_times_nt(table, x):
+    both = dot_nt(table, x)
+    rows = table.shape[0] // 2
+    return both[:rows] + both[rows:]
+
+
+def spread(x, rows):
+    high, low = split(x)
+    high, low = high.astype(F32), low.astype(F32)
+    for y in range(P_SIZE):
+        part = slice(y * 32, y * 32 + 32)
+        rows[pl.ds(y, x.shape[0], stride=P_SIZE), :] = jnp.concatenate([high[:, part], low[:, part]], axis=1)
+    return rows[...].astype(BF16)
 
 
 def stacked(x, width):
@@ -214,49 +297,47 @@
     return lax.broadcasted_iota(jnp.int32, (rows, 128), 1)
 
 
-class Loaded:
-    def __init__(self, names, sources, targets, sem):
-        self.refs = dict(zip(names, targets))
-        self.copies = {
-            name: pltpu.make_async_copy(source, target, sem.at[i])
-            for i, (name, source, target) in enumerate(zip(names, sources, targets))
-        }
-        for name in names:
-            self.copies[name].start()
-
-    def __getitem__(self, name):
-        if name in self.copies:
-            self.copies.pop(name).wait()
-        return self.refs[name]
-
-
-def kind(name):
-    table = tables()[name]
-    dims = table.shape[1:] if name in ("xa", "ey", "ex") else table.shape
-    return dims, F32 if table.dtype == np.float32 else BF16
-
-
-A_TABLES = ("sc", "bd", "rm", "ty", "tz", "tx1", "u", "k1", "tx2", "tx3", "kl", "s32", "bd32")
-B_TABLES = ("yb", "xa", "wc", "ey", "ex")
-C_TABLES = ("lz", "sel", "sbz", "tz2", "rm32", "s32", "bd32")
-LATER = B_TABLES + C_TABLES
-
-
-def first_kernel(q_ref, *refs):
-    n, later = len(A_TABLES), len(LATER)
-    own_tables, later_tables, refs = refs[:n], refs[n : n + later], refs[n + later :]
-    m_ref, own_ref, spec_ref = refs[:3]
-    fetched, refs = refs[3 : 3 + later], refs[3 + later :]
-    rows, rows32, ls, lp, ly, spill = refs[:6]
-    t = Loaded(A_TABLES, own_tables, refs[6 : 6 + n], refs[6 + n])
-    place = {"xa": lax.axis_index("gs"), "ey": lax.axis_index("gy"), "ex": lax.axis_index("gc")}
-    sources = [ref.at[place[k]] if k in place else ref for k, ref in zip(LATER, later_tables)]
-    ahead = Loaded(LATER, sources, fetched, refs[7 + n])
-    x = table_times(t["sc"], q_ref[...])
-    for y in range(P_SIZE):
-        rows[pl.ds(y, 64, stride=P_SIZE), :] = x[:, y * 32 : y * 32 + 32]
-    x = table_times(t["sc"], rows[...], dot_nt)
-    x = times_table(stacked(x, 128), t["bd"]) * t["rm"][...]
+SOURCES = ("rm", "wide", "small", "xa", "ey", "ex", "later", "scales")
+KEPT = (((2, 256, 128), BF16), ((2, 256, 256), BF16), ((2, 128, 512), BF16), ((2, 192, 256), BF16), ((2, 128, 1408), BF16), ((768, 256), F32))
+
+
+def first_kernel(q_hbm, rm_hbm, wide_hbm, small_hbm, xa_hbm, ey_hbm, ex_hbm, later_hbm, scales_hbm,
+                 m_ref, own_ref, spec_ref, small, xa, ey, ex, later, scales,
+                 q, rm, wide, rows, rows32, ls, lp, ly, spill, sem):
+    started = []
+
+    def start(source, target):
+        copy = pltpu.make_async_copy(source, target, sem.at[len(started)])
+        started.append(copy)
+        copy.start()
+        return copy
+
+    def part(first, last):
+        return start(wide_hbm.at[:, first:last, :], wide.at[:, first:last, :])
+
+    now = [start(q_hbm, q), start(small_hbm, small), part(0, 512)]
+    soon = [start(rm_hbm, rm)]
+    for copy in now:
+        copy.wait()
+    soon += [part(512, 1792), part(1792, 3328)]
+    t = {name: View(wide, row, count, 0, 256) for name, (row, count) in WIDE.items()}
+    x = row_times(small_table(small, "sc|"), q[...])
+    x = block_times_nt(small_table(small, "sc="), spread(x, rows))
+    x = times_table(stacked(x, 128), t["bd"])
+    bd32 = View(small, 128, 128, 0, 128)
+    y = row_times(small_table(small, "s32|"), q[...])
+    y = block_times_nt(small_table(small, "s32="), spread(y, rows32))
+    spec_ref[...] = times_table(stacked(y, 128), bd32)
+    for copy in soon:
+        copy.wait()
+    ahead = [
+        start(xa_hbm.at[lax.axis_index("gs")], xa),
+        start(ey_hbm.at[lax.axis_index("gy")], ey),
+        start(ex_hbm.at[lax.axis_index("gc")], ex),
+        start(scales_hbm, scales),
+        start(later_hbm, later),
+    ]
+    x = x * rm[...]
     x = times_table(x, t["ty"])
     for i in range(4):
         z = table_times(t["tz"], x[i * 256 : i * 256 + 256])
@@ -267,14 +348,9 @@
             ly[:, k * 16 : k * 16 + 16] = z[j * 32 + 16 : j * 32 + 32, 128:144]
     samples = times_table(ls[...], t["tx1"])
     coefs = times_table(lp[...], t["tx2"]) + times_table(ly[...], t["tx3"])
-    x = table_times(t["u"], samples)
+    x = row_times(small_table(small, "u|"), samples)
     coefs = coefs - times_table(x[16:32], t["kl"])
     own_ref[...] = coefs[:, 0:128]
-    y = table_times(t["s32"], q_ref[...])
-    for i in range(P_SIZE):
-        rows32[pl.ds(i, 32, stride=P_SIZE), :] = y[:, i * 32 : i * 32 + 32]
-    y = table_times(t["s32"], rows32[...], dot_nt)
-    spec_ref[...] = times_table(stacked(y, 128), t["bd32"])
     x = (times_table(x[0:8], t["k1"]) + x[8:16]).T
     for i in range(16):
         spill[:, i * 8 : i * 8 + 8] = x[i * 16 : i * 16 + 16]
@@ -283,8 +359,8 @@
     for i in range(16):
         m_ref[i * 24 : i * 24 + 16, :] = spilled
         m_ref[i * 24 + 16 : i * 24 + 24, :] = tile
-    for name in LATER:
-        ahead[name]
+    for copy in ahead:
+        copy.wait()
 
 
 def unpacked(tile, source, slot):
@@ -295,20 +371,18 @@
     return jnp.where(lanes(NL) // 16 == slot, jnp.concatenate(parts, axis=0), 0.0)
 
 
-def strip_kernel(got_ref, own_ref, *refs):
-    t = dict(zip(B_TABLES, refs))
-    m_ref, coefs_ref = refs[len(B_TABLES) :]
+def strip_kernel(got_ref, own_ref, xa, ey, ex, later, scales, m_ref, coefs_ref):
     s, c, b = lax.axis_index("gs"), lax.axis_index("gc"), lax.axis_index("gy")
     source = [
         jnp.concatenate([got_ref[(i * 8 + j) * 24 : (i * 8 + j) * 24 + 16, :] for j in range(N_GY)], axis=0)
         for i in range(2)
     ]
-    x = table_times(t["yb"], jnp.concatenate(source, axis=1))
+    x = table_times(View(later, 0, 64, 1024, 128), jnp.concatenate(source, axis=1))
     lane = lax.broadcasted_iota(jnp.int32, (64, 256), 1)
     x = jnp.concatenate([jnp.where(lane % 8 == k, x, 0.0) for k in range(CELLS)], axis=0)
-    x = times_table(x, t["xa"]) * t["wc"][...]
-    x = table_times(t["ey"], x)
-    x = table_times(t["ex"], x, dot_nt)
+    x = times_table(x, xa) * scales[0:512, :]
+    x = table_times(ey, x)
+    x = table_times(ex, x, dot_nt)
     m_ref[...] = jnp.zeros((128, 128), F32)
     lane = lanes(16)
     for f in range(2):
@@ -340,24 +414,26 @@
     coefs_ref[...] = coefs
 
 
-def last_kernel(m_ref, coefs_ref, spec_ref, *refs):
-    t = dict(zip(C_TABLES, refs))
-    out_ref, rows, flat = refs[len(C_TABLES) :]
+def last_kernel(m_ref, coefs_ref, spec_ref, small, later, scales, out_ref, rows, flat):
+    s32, bd32 = small_table(small, "s32|"), View(small, 128, 128, 0, 128)
     got = jnp.sum(m_ref[...].reshape(16, 8, 128), axis=0)
     coefs = coefs_ref[...] + jnp.where(lax.axis_index("gc") == 0, unpacked(got, 96, 0), unpacked(got, 96, 1))
-    lz = t["lz"][...]
-    sel = t["sel"][...]
+    lz = scales[512:544, 128:256]
     high, low = split(jnp.concatenate([lz * got[i : i + 1] for i in range(4)], axis=1))
-    x = dot(high, sel) + dot(low, sel) + table_times(t["sbz"], coefs)
-    x = times_table(x, t["tz2"])
-    x = (stacked(x, 128) + spec_ref[...]) * t["rm32"][...]
-    x = table_times(t["s32"], unstacked(x, 32))
-    x = times_table(stacked(x, 128), t["bd32"])
+    x = row_times(later[0, 64:96, 1024:1072], coefs)
+    for i in range(4):
+        part = jnp.concatenate([high[:, i * 128 : i * 128 + 128], low[:, i * 128 : i * 128 + 128]], axis=0)
+        part = dot(part, later[i // 2, :, 1152 + i % 2 * 128 : 1280 + i % 2 * 128])
+        x = x + part[:32] + part[32:]
+    x = times_table(x, View(later, 0, 128, 0, 1024))
+    x = (stacked(x, 128) + spec_ref[...]) * scales[512:768, 0:128]
+    x = row_times(s32, unstacked(x, 32))
+    x = times_table(stacked(x, 128), bd32)
     for i in range(8):
         rows[i * 128 : i * 128 + 128, :] = x[i * 32 : i * 32 + 32].T
     for y in range(P_SIZE):
         flat[:, y * 32 : y * 32 + 32] = rows[pl.ds(y, 32, stride=P_SIZE), :]
-    out_ref[...] = table_times(t["s32"], flat[...])
+    out_ref[...] = row_times(s32, flat[...])
 
 
 def vmem(count):
@@ -377,45 +453,47 @@
 
 
 def body(charge):
-    t = {k: jnp.asarray(v) for k, v in tables().items()}
-    message, own, spec, *fetched = pl.pallas_call(
+    t = packs()
+    sources = [charge] + [jnp.asarray(t[k]) for k in SOURCES]
+    message, own, spec, small, xa, ey, ex, later, scales = pl.pallas_call(
         first_kernel,
-        out_shape=[shape(384, 128), shape(NL, 128), shape(256, 128)] + [jax.ShapeDtypeStruct(*kind(k)) for k in LATER],
-        in_specs=vmem(1) + hbm(len(A_TABLES) + len(LATER)),
-        out_specs=vmem(3 + len(LATER)),
+        out_shape=[shape(384, 128), shape(NL, 128), shape(256, 128)] + [jax.ShapeDtypeStruct(*k) for k in KEPT],
+        in_specs=hbm(len(sources)),
+        out_specs=vmem(3 + len(KEPT)),
         scratch_shapes=[
-            pltpu.VMEM((2048, 32), F32),
-            pltpu.VMEM((1024, 32), F32),
+            pltpu.VMEM((32, 1024), F32),
+            pltpu.VMEM((1024, 256), F32),
+            pltpu.VMEM((2, 3328, 256), BF16),
+            pltpu.VMEM((2048, 64), F32),
+            pltpu.VMEM((1024, 64), F32),
             pltpu.VMEM((16, 1024), F32),
             pltpu.VMEM((16, 1024), F32),
             pltpu.VMEM((16, 256), F32),
             pltpu.VMEM((16, 128), F32),
-        ]
-        + [pltpu.VMEM(*kind(k)) for k in A_TABLES]
-        + [pltpu.SemaphoreType.DMA((len(A_TABLES),)), pltpu.SemaphoreType.DMA((len(LATER),))],
+            pltpu.SemaphoreType.DMA((11,)),
+        ],
         compiler_params=params(24),
         name="first",
-    )(*[pltpu.with_memory_space_constraint(v, pltpu.HBM) for v in (charge, *[t[k] for k in A_TABLES + LATER])])
-    fetched = dict(zip(LATER, fetched))
+    )(*[pltpu.with_memory_space_constraint(v, pltpu.HBM) for v in sources])
     strip = lax.all_to_all(message.reshape(16, 24, 128), ("gc", "gy"), 0, 0).reshape(384, 128)
     message, coefs = pl.pallas_call(
         strip_kernel,
         out_shape=(shape(128, 128), shape(NL, 128)),
-        in_specs=vmem(2 + len(B_TABLES)),
+        in_specs=vmem(7),
         out_specs=tuple(vmem(2)),
         compiler_params=params(12),
         name="strip",
-    )(strip, own, *[fetched[k] for k in B_TABLES])
+    )(strip, own, xa, ey, ex, later, scales)
     arrived = lax.all_to_all(message.reshape(16, 8, 128), "gs", 0, 0).reshape(128, 128)
     return pl.pallas_call(
         last_kernel,
         out_shape=shape(32, 1024),
-        in_specs=vmem(3 + len(C_TABLES)),
+        in_specs=vmem(6),
         out_specs=vmem(1)[0],
         scratch_shapes=[pltpu.VMEM((1024, 32), F32), pltpu.VMEM((32, 1024), F32)],
         compiler_params=params(12),
         name="last",
-    )(arrived, coefs, spec, *[fetched[k] for k in C_TABLES])
+    )(arrived, coefs, spec, small, later, scales)
 
 
 def solution(mesh):

time: 45.5 us -> 43.1 us (0.947)
  Pallas kernels: 12.7 us -> 10.1 us
    pallas_call x1, Pallas kernels: 9.15 us -> 6.81 us  [body(): pl.pallas_call(first_kernel, out_shape=[shape(384, 128), shape(NL, 128),...]
where the time goes in v2:
time: 43.1 us; the launch traced here: 42.8 us
  blocking collectives  32.7 us (76%)
  Pallas kernels  10.1 us (23%)
    all_to_all x1, blocking collectives, body(): lax.all_to_all(message.reshape(16, 8, 128), 'gs', 0, 0).reshape(128, 128)  19.4 us
    all_to_all x1, blocking collectives, body(): lax.all_to_all(message.reshape(16, 24, 128), ('gc', 'gy'), 0, 0)  13.3 us
    pallas_call x1, Pallas kernels, body(): pl.pallas_call(first_kernel, out_shape=[shape(384, 128), shape(NL, 128),...  6.81 us
    pallas_call x1, Pallas kernels, body(): pl.pallas_call(last_kernel, out_shape=shape(32, 1024), in_specs=vmem(6),...  1.98 us
    pallas_call x1, Pallas kernels, body(): pl.pallas_call(strip_kernel, out_shape=(shape(128, 128), shape(NL, 128)),...  1.35 us

profile of v2, /device:TPU:1, one launch (start us, length us, event | category | flops | bytes accessed | tf_op | source)
XLA Modules:
  0.0 42.8 jit_solution(2658062549620002336)
XLA Ops:
  0.0 6.8 %first.1 = (f32[384,128]{1,0:T(8,128)S(1)}, f32[16,128]{1,0:T(8,128)S(1)}, f32[256,128]{1,0:T(8,128)S(1)}, bf16[2,256,128]{2,1,0:T(8,128)(2,1)S(1)}, bf16[2,256,...) custom-call(f32[32,1024]{1,0:T(8,128)} %q_hbm.1, ...), custom_call_target="tpu_custom_call" | custom-call | tf_op jit(solution)/shard_map/first/pallas_call | solution.py:458
  6.8 13.3 %all_to_all.10 = f32[16,24,128]{2,1,0:T(8,128)S(1)} all-to-all(f32[16,24,128]{2,1,0:T(8,128)S(1)} %bitcast.6), channel_id=1, replica_groups=mesh['gs'=16,'gc'=2,'gy'=8] {'gc','gy'}, dimensions={0} | all-to-all | bytes 393216 | tf_op jit(solution)/shard_map/all_to_all | solution.py:478
  20.1 1.4 %strip.1 = (f32[128,128]{1,0:T(8,128)S(1)}, f32[16,128]{1,0:T(8,128)S(1)}) custom-call(f32[384,128]{1,0:T(8,128)S(1)} %bitcast.4, f32[16,128]{1,0:T(8,128)S(1)} %get-tuple-element.17.own_ref, bf16[2,256,256]{2,1,0:T(8,128)(2,1)S(1)} %get-tuple-element.18.xa, bf16[2,128,512]{2,1,0:T(8,128)(2,1)S(1)} %get-tuple-element.19.ey, ...), custom_call_target="tpu_custom_call" | custom-call | tf_op jit(solution)/shard_map/strip/pallas_call | solution.py:479
  21.5 19.4 %all_to_all.11 = f32[16,8,128]{2,1,0:T(8,128)S(1)} all-to-all(f32[16,8,128]{2,1,0:T(8,128)S(1)} %bitcast.7), channel_id=1, replica_groups=mesh['gs'=16,'gc'=2,'gy'=8] {'gs'}, dimensions={0} | all-to-all | bytes 131072 | tf_op jit(solution)/shard_map/all_to_all | solution.py:487
  40.9 2.0 %last.1 = f32[32,1024]{1,0:T(8,128)} custom-call(f32[128,128]{1,0:T(8,128)S(1)} %bitcast.5, f32[16,128]{1,0:T(8,128)S(1)} %get-tuple-element.24.coefs_ref, f32[256,128]{1,0:T(8,128)S(1)} %get-tuple-element.25.spec_ref, bf16[2,256,128]{2,1,0:T(8,128)(2,1)S(1)} %get-tuple-element.26.small, bf16[2,128,1408]{2,1,0:T(8,128)(2,1)S(1)} %get-tuple-element.21.later, ...), custom_call_target="tpu_custom_call" | custom-call | tf_op jit(solution)/shard_map/last/pallas_call | solution.py:488

commit v3 on v2

--- a/solution.py
+++ b/solution.py
@@ -92,13 +92,14 @@
     st = s64[places]
     bl = basis.T @ fine[inside]
     lt = fine[places]
-    lanes_x, lanes_y = [[0], [16], [128, 144], [160, 176]], [[32], [48], [192, 208], [224, 240]]
+    lanes_x, lanes_y = [0, 16, 64, 80], [32, 48, 96, 112]
     sc = s64[:, inside]
     t["sc"] = pair(sc)
     t["bd"] = pair(np.kron(eye(4), sc.T))
-    kx = m64.reshape(16, 1, 4, 1)
-    rm = (2.0 / (n + 1)) ** 3 / (kx + m64.reshape(1, n, 1, 1) + m64.reshape(1, 1, 1, n))
-    t["rm"] = rm.reshape(16 * n, 4 * n).astype(np.float32)
+    mu = np.zeros((16 + n, 256))
+    mu[:16] = (m64.reshape(16, 4, 1) + m64).reshape(16, 256)
+    mu[16:] = m64[:, None]
+    t["mu"] = (mu * ((n + 1) / 2.0) ** 3).astype(np.float32)
     ty = np.zeros((4, n, 256))
     for i in range(4):
         ty[i, :, i * 16 : i * 16 + 16] = r.T
@@ -107,19 +108,18 @@
     t["ty"] = pair(ty.reshape(4 * n, 256))
     t["tz"] = pair(np.kron(eye(4), np.concatenate([r, bs], axis=0)))
     t["tx1"] = pair(np.kron(r.T, eye(16)))
-    tx2 = np.zeros((n, NL, 256))
-    tx3 = np.zeros((n, 4, 256))
-    kl = np.zeros((16, 16, 256))
+    tx2 = np.zeros((n, NL, 128))
+    tx3 = np.zeros((n, 4, 128))
+    kl = np.zeros((16, 16, 128))
     for i in range(4):
-        for lane in lanes_x[i]:
-            tx2[:, :, lane : lane + NL] = st[i][:, None, None] * eye(NL)
-            kl[:, :, lane : lane + NL] = lt[i][:, None, None] * bl.T[None]
-        for lane in lanes_y[i]:
-            tx3[:, i, lane : lane + NL] = bs.T
-            kl[:, :, lane : lane + NL] = bl.T[:, None, :] * lt[i][None, :, None]
-    t["tx2"] = pair(tx2.reshape(n * NL, 256))
-    t["tx3"] = pair(tx3.reshape(n * 4, 256))
-    t["kl"] = pair(kl.reshape(256, 256))
+        at_x, at_y = slice(lanes_x[i], lanes_x[i] + NL), slice(lanes_y[i], lanes_y[i] + NL)
+        tx2[:, :, at_x] = st[i][:, None, None] * eye(NL)
+        kl[:, :, at_x] = lt[i][:, None, None] * bl.T[None]
+        tx3[:, i, at_y] = bs.T
+        kl[:, :, at_y] = bl.T[:, None, :] * lt[i][None, :, None]
+    t["tx2"] = pair(tx2.reshape(n * NL, 128))
+    t["tx3"] = pair(tx3.reshape(n * 4, 128))
+    t["kl"] = pair(kl.reshape(256, 128))
     first = W // Q
     u1 = np.zeros((CELLS, 16))
     u2 = np.zeros((CELLS, 16))
@@ -179,7 +179,17 @@
     return t
 
 
-WIDE = {"bd": (0, 128), "ty": (128, 256), "tz": (384, 128), "tx1": (512, 1024), "k1": (1536, 256), "tx2": (1792, 1024), "tx3": (2816, 256), "kl": (3072, 256)}
+WIDE = {
+    "bd": (0, 128, 0, 256),
+    "ty": (128, 256, 0, 256),
+    "tz": (384, 128, 0, 256),
+    "tx1": (512, 1024, 0, 256),
+    "k1": (1536, 256, 0, 256),
+    "tx2a": (1792, 512, 0, 128),
+    "tx2b": (1792, 512, 128, 128),
+    "tx3": (2304, 256, 0, 128),
+    "kl": (2304, 256, 128, 128),
+}
 SMALL = {"sc|": (0, 0, 64, 0, 96), "s32|": (0, 64, 32, 0, 96), "u|": (0, 96, 32, 0, 48), "sc=": (1, 0, 128, 0, 64), "s32=": (1, 0, 64, 64, 64)}
 
 
@@ -199,6 +209,10 @@
         form = in_row if name[-1] == "|" else in_block
         small[which, row : row + rows, lane : lane + width] = form(t[name[:-1]])
     small[:, 128:256] = t["bd32"]
+    parts = {**t, "tx2a": t["tx2"][:, :512], "tx2b": t["tx2"][:, 512:]}
+    wide = np.zeros((2, 2560, 256), ml_dtypes.bfloat16)
+    for name, (row, rows, lane, width) in WIDE.items():
+        wide[:, row : row + rows, lane : lane + width] = parts[name]
     later = np.zeros((2, 128, 1408), ml_dtypes.bfloat16)
     later[:, :, :1024] = t["tz2"]
     later[:, :64, 1024:1152] = t["yb"]
@@ -210,8 +224,8 @@
     scales[512:544, 128:] = t["lz"]
     return {
         "small": small,
-        "wide": np.concatenate([t[name] for name in WIDE], axis=1),
-        "rm": t["rm"],
+        "wide": wide,
+        "mu": t["mu"],
         "xa": t["xa"],
         "ey": t["ey"],
         "ex": t["ex"],
@@ -297,13 +311,26 @@
     return lax.broadcasted_iota(jnp.int32, (rows, 128), 1)
 
 
-SOURCES = ("rm", "wide", "small", "xa", "ey", "ex", "later", "scales")
+FIRST = ("mu", "wide", "small")
+NEXT = ("small", "xa", "ey", "ex", "later", "scales")
 KEPT = (((2, 256, 128), BF16), ((2, 256, 256), BF16), ((2, 128, 512), BF16), ((2, 192, 256), BF16), ((2, 128, 1408), BF16), ((768, 256), F32))
 
 
-def first_kernel(q_hbm, rm_hbm, wide_hbm, small_hbm, xa_hbm, ey_hbm, ex_hbm, later_hbm, scales_hbm,
-                 m_ref, own_ref, spec_ref, small, xa, ey, ex, later, scales,
-                 q, rm, wide, rows, rows32, ls, lp, ly, spill, sem):
+def fetch_kernel(after_ref, *refs):
+    places = {1: lax.axis_index("gs"), 2: lax.axis_index("gy"), 3: lax.axis_index("gc")}
+    n = len(NEXT)
+    copies = [
+        pltpu.make_async_copy(source.at[places[i]] if i in places else source, target, refs[-1].at[i])
+        for i, (source, target) in enumerate(zip(refs[:n], refs[n : 2 * n]))
+    ]
+    for copy in copies:
+        copy.start()
+    for copy in copies:
+        copy.wait()
+
+
+def first_kernel(q_hbm, mu_hbm, wide_hbm, small_hbm, m_ref, own_ref, spec_ref,
+                 q, mu, wide, small, rows, rows32, ls, lp, ly, spill, sem):
     started = []
 
     def start(source, target):
@@ -315,12 +342,11 @@
     def part(first, last):
         return start(wide_hbm.at[:, first:last, :], wide.at[:, first:last, :])
 
-    now = [start(q_hbm, q), start(small_hbm, small), part(0, 512)]
-    soon = [start(rm_hbm, rm)]
+    now = [start(q_hbm, q), start(small_hbm, small), part(0, 512), start(mu_hbm, mu)]
     for copy in now:
         copy.wait()
-    soon += [part(512, 1792), part(1792, 3328)]
-    t = {name: View(wide, row, count, 0, 256) for name, (row, count) in WIDE.items()}
+    soon = [part(512, 1536), part(1536, 2560)]
+    t = {name: View(wide, *place) for name, place in WIDE.items()}
     x = row_times(small_table(small, "sc|"), q[...])
     x = block_times_nt(small_table(small, "sc="), spread(x, rows))
     x = times_table(stacked(x, 128), t["bd"])
@@ -328,16 +354,7 @@
     y = row_times(small_table(small, "s32|"), q[...])
     y = block_times_nt(small_table(small, "s32="), spread(y, rows32))
     spec_ref[...] = times_table(stacked(y, 128), bd32)
-    for copy in soon:
-        copy.wait()
-    ahead = [
-        start(xa_hbm.at[lax.axis_index("gs")], xa),
-        start(ey_hbm.at[lax.axis_index("gy")], ey),
-        start(ex_hbm.at[lax.axis_index("gc")], ex),
-        start(scales_hbm, scales),
-        start(later_hbm, later),
-    ]
-    x = x * rm[...]
+    x = jnp.concatenate([x[i * 64 : i * 64 + 64] / (mu[16:80, :] + mu[i : i + 1, :]) for i in range(16)], axis=0)
     x = times_table(x, t["ty"])
     for i in range(4):
         z = table_times(t["tz"], x[i * 256 : i * 256 + 256])
@@ -346,21 +363,25 @@
             ls[:, k * 64 : k * 64 + 64] = z[j * 32 : j * 32 + 16, 0:64]
             lp[:, k * 64 : k * 64 + 64] = z[j * 32 + 16 : j * 32 + 32, 64:128]
             ly[:, k * 16 : k * 16 + 16] = z[j * 32 + 16 : j * 32 + 32, 128:144]
+    for copy in soon:
+        copy.wait()
     samples = times_table(ls[...], t["tx1"])
-    coefs = times_table(lp[...], t["tx2"]) + times_table(ly[...], t["tx3"])
+    coefs = times_table(lp[:, 0:512], t["tx2a"]) + times_table(lp[:, 512:1024], t["tx2b"]) + times_table(ly[...], t["tx3"])
     x = row_times(small_table(small, "u|"), samples)
     coefs = coefs - times_table(x[16:32], t["kl"])
-    own_ref[...] = coefs[:, 0:128]
+    own_ref[...] = coefs
     x = (times_table(x[0:8], t["k1"]) + x[8:16]).T
     for i in range(16):
         spill[:, i * 8 : i * 8 + 8] = x[i * 16 : i * 16 + 16]
     spilled = spill[...]
-    tile = jnp.where(lanes(8) // 16 % 2 == 0, coefs[0:8, 128:256], coefs[8:16, 128:256])
+    tile = jnp.zeros((8, 128), F32)
+    for i in range(8):
+        value = coefs[i % 2 * 8 : i % 2 * 8 + 8]
+        shift = (16 * i - 64 - i // 2 * 16) % 128
+        tile = jnp.where(lanes(8) // 16 == i, pltpu.roll(value, shift, 1) if shift else value, tile)
     for i in range(16):
         m_ref[i * 24 : i * 24 + 16, :] = spilled
         m_ref[i * 24 + 16 : i * 24 + 24, :] = tile
-    for copy in ahead:
-        copy.wait()
 
 
 def unpacked(tile, source, slot):
@@ -453,28 +474,37 @@
 
 
 def body(charge):
-    t = packs()
-    sources = [charge] + [jnp.asarray(t[k]) for k in SOURCES]
-    message, own, spec, small, xa, ey, ex, later, scales = pl.pallas_call(
+    t = {k: pltpu.with_memory_space_constraint(jnp.asarray(v), pltpu.HBM) for k, v in packs().items()}
+    message, own, spec = pl.pallas_call(
         first_kernel,
-        out_shape=[shape(384, 128), shape(NL, 128), shape(256, 128)] + [jax.ShapeDtypeStruct(*k) for k in KEPT],
-        in_specs=hbm(len(sources)),
-        out_specs=vmem(3 + len(KEPT)),
+        out_shape=[shape(384, 128), shape(NL, 128), shape(256, 128)],
+        in_specs=hbm(4),
+        out_specs=vmem(3),
         scratch_shapes=[
             pltpu.VMEM((32, 1024), F32),
-            pltpu.VMEM((1024, 256), F32),
-            pltpu.VMEM((2, 3328, 256), BF16),
+            pltpu.VMEM((80, 256), F32),
+            pltpu.VMEM((2, 2560, 256), BF16),
+            pltpu.VMEM((2, 256, 128), BF16),
             pltpu.VMEM((2048, 64), F32),
             pltpu.VMEM((1024, 64), F32),
             pltpu.VMEM((16, 1024), F32),
             pltpu.VMEM((16, 1024), F32),
             pltpu.VMEM((16, 256), F32),
             pltpu.VMEM((16, 128), F32),
-            pltpu.SemaphoreType.DMA((11,)),
+            pltpu.SemaphoreType.DMA((6,)),
         ],
         compiler_params=params(24),
         name="first",
-    )(*[pltpu.with_memory_space_constraint(v, pltpu.HBM) for v in sources])
+    )(pltpu.with_memory_space_constraint(charge, pltpu.HBM), *[t[k] for k in FIRST])
+    small, xa, ey, ex, later, scales = pl.pallas_call(
+        fetch_kernel,
+        out_shape=[jax.ShapeDtypeStruct(*k) for k in KEPT],
+        in_specs=hbm(1 + len(NEXT)),
+        out_specs=vmem(len(KEPT)),
+        scratch_shapes=[pltpu.SemaphoreType.DMA((len(NEXT),))],
+        compiler_params=params(12),
+        name="fetch",
+    )(own, *[t[k] for k in NEXT])
     strip = lax.all_to_all(message.reshape(16, 24, 128), ("gc", "gy"), 0, 0).reshape(384, 128)
     message, coefs = pl.pallas_call(
         strip_kernel,

time: 43.1 us -> 42.3 us (0.981)
  blocking collectives: 32.7 us -> 19.4 us
  starting transfers between devices: 0 us -> 6.84 us
  waiting for transfers between devices: 0 us -> 4.95 us
  Pallas kernels: 10.1 us -> 10.9 us
    all_to_all x1 -> x0, blocking collectives: 13.3 us -> none  [body(): lax.all_to_all(message.reshape(16, 24, 128), ('gc', 'gy'), 0, 0)]
    all_to_all x0 -> x1, starting transfers between devices: none -> 6.84 us  [body(): lax.all_to_all(message.reshape(16, 24, 128), ('gc', 'gy'), 0, 0)]
    all_to_all x0 -> x1, waiting for transfers between devices: none -> 4.95 us  [body(): lax.all_to_all(message.reshape(16, 24, 128), ('gc', 'gy'), 0, 0)]
    pallas_call x0 -> x1, Pallas kernels: none -> 1.7 us  [body(): pl.pallas_call(fetch_kernel, out_shape=[jax.ShapeDtypeStruct(*k) for k in...]
    pallas_call x1, Pallas kernels: 6.81 us -> 5.84 us  [body(): pl.pallas_call(first_kernel, out_shape=[shape(384, 128), shape(NL, 128),...]
  transfers between devices with their start and end apart: 0 -> 1, of which waited for: 0 -> 1; matrix products, arithmetic and copies ran while one was open for 0% -> 0% of each run, Pallas kernels for 0% -> 4%
where the time goes in v3:
time: 42.3 us; the launch traced here: 42.1 us
  blocking collectives  19.4 us (46%)
  Pallas kernels  10.9 us (26%)
  starting transfers between devices  6.84 us (16%)
  waiting for transfers between devices  4.95 us (12%)
    all_to_all x1, blocking collectives, body(): lax.all_to_all(message.reshape(16, 8, 128), 'gs', 0, 0).reshape(128, 128)  19.4 us
    all_to_all x1, starting transfers between devices, body(): lax.all_to_all(message.reshape(16, 24, 128), ('gc', 'gy'), 0, 0)  6.84 us
    pallas_call x1, Pallas kernels, body(): pl.pallas_call(first_kernel, out_shape=[shape(384, 128), shape(NL, 128),...  5.84 us
    all_to_all x1, waiting for transfers between devices, body(): lax.all_to_all(message.reshape(16, 24, 128), ('gc', 'gy'), 0, 0)  4.95 us
    pallas_call x1, Pallas kernels, body(): pl.pallas_call(last_kernel, out_shape=shape(32, 1024), in_specs=vmem(6),...  1.98 us
    pallas_call x1, Pallas kernels, body(): pl.pallas_call(fetch_kernel, out_shape=[jax.ShapeDtypeStruct(*k) for k in...  1.7 us
    pallas_call x1, Pallas kernels, body(): pl.pallas_call(strip_kernel, out_shape=(shape(128, 128), shape(NL, 128)),...  1.35 us
  transfers between devices with their start and end apart: 1, of which 1 were waited for; matrix products, arithmetic and copies ran while one was open for 0% of the time, Pallas kernels for 4%

profile of v3, /device:TPU:1, one launch (start us, length us, event | category | flops | bytes accessed | tf_op | source)
XLA Modules:
  0.0 42.1 jit_solution(4382809303556085885)
XLA Ops:
  0.0 5.8 %first.1 = (f32[384,128]{1,0:T(8,128)}, f32[16,128]{1,0:T(8,128)S(1)}, f32[256,128]{1,0:T(8,128)S(1)}) custom-call(f32[32,1024]{1,0:T(8,128)} %q_hbm.1, f32[80,256]{1,0:T(8,128)} %constant.18.clone.mu_hbm, bf16[2,2560,256]{2,1,0:T(8,128)(2,1)} %constant.17.clone.wide_hbm, bf16[2,256,128]{2,1,0:T(8,128)(2,1)} %constant.16.clone.small_hbm.refs_0_), custom_call_target="tpu_custom_call" | custom-call | tf_op jit(solution)/shard_map/first/pallas_call | solution.py:478
  5.8 6.8 %all-to-all-start = ((f32[16,24,128]{2,1,0:T(8,128)}), f32[16,24,128]{2,1,0:T(8,128)S(1)}, u32[]{:S(2)}, u32[]{:S(2)}) async-start(f32[16,24,128]{2,1,0:T(8,128)} %bitcast), calls=%async_computation | async-start | bytes 393216 | tf_op jit(solution)/shard_map/all_to_all | solution.py:508
  12.7 1.7 %fetch.1 = (bf16[2,256,128]{2,1,0:T(8,128)(2,1)S(1)}, bf16[2,256,256]{2,1,0:T(8,128)(2,1)S(1)}, bf16[2,128,512]{2,1,0:T(8,128)(2,1)S(1)}, bf16[2,192,256]{2,1,0:...) custom-call(f32[16,128]{1,0:T(8,128)S(1)} %get-tuple-element.17.after_ref.own_ref, ...), custom_call_target="tpu_custom_call" | custom-call | tf_op jit(solution)/shard_map/fetch/pallas_call | solution.py:499
  14.4 4.9 %all-to-all-done = f32[16,24,128]{2,1,0:T(8,128)S(1)} async-done(((f32[16,24,128]{2,1,0:T(8,128)}), f32[16,24,128]{2,1,0:T(8,128)S(1)}, u32[]{:S(2)}, u32[]{:S(2)}) %all-to-all-start) | async-done | bytes 196640 | tf_op jit(solution)/shard_map/all_to_all | solution.py:508
  19.3 1.4 %strip.1 = (f32[128,128]{1,0:T(8,128)S(1)}, f32[16,128]{1,0:T(8,128)S(1)}) custom-call(f32[384,128]{1,0:T(8,128)S(1)} %bitcast.4, f32[16,128]{1,0:T(8,128)S(1)} %get-tuple-element.17.after_ref.own_ref, bf16[2,256,256]{2,1,0:T(8,128)(2,1)S(1)} %get-tuple-element.18.xa, bf16[2,128,512]{2,1,0:T(8,128)(2,1)S(1)} %get-tuple-element.19.ey, ...), custom_call_target="tpu_custom_call" | custom-call | tf_op jit(solution)/shard_map/strip/pallas_call | solution.py:509
  20.7 19.4 %all_to_all.10 = f32[16,8,128]{2,1,0:T(8,128)S(1)} all-to-all(f32[16,8,128]{2,1,0:T(8,128)S(1)} %bitcast.6), channel_id=1, replica_groups=mesh['gs'=16,'gc'=2,'gy'=8] {'gs'}, dimensions={0} | all-to-all | bytes 131072 | tf_op jit(solution)/shard_map/all_to_all | solution.py:517
  40.1 2.0 %last.1 = f32[32,1024]{1,0:T(8,128)} custom-call(f32[128,128]{1,0:T(8,128)S(1)} %bitcast.5, f32[16,128]{1,0:T(8,128)S(1)} %get-tuple-element.24.coefs_ref, f32[256,128]{1,0:T(8,128)S(1)} %get-tuple-element.25.spec_ref, bf16[2,256,128]{2,1,0:T(8,128)(2,1)S(1)} %get-tuple-element.26.small, bf16[2,128,1408]{2,1,0:T(8,128)(2,1)S(1)} %get-tuple-element.21.later, ...), custom_call_target="tpu_custom_call" | custom-call | tf_op jit(solution)/shard_map/last/pallas_call | solution.py:518
Async XLA Ops:
  5.8 13.5 %all-to-all-start = ((f32[16,24,128]{2,1,0:T(8,128)}), f32[16,24,128]{2,1,0:T(8,128)S(1)}, u32[]{:S(2)}, u32[]{:S(2)}) async-start(f32[16,24,128]{2,1,0:T(8,128)} %bitcast), calls=%async_computation | async-start | bytes 393216 | tf_op jit(solution)/shard_map/all_to_all | solution.py:508

commit v4 on v3

--- a/solution.py
+++ b/solution.py
@@ -293,10 +293,12 @@
 def spread(x, rows):
     high, low = split(x)
     high, low = high.astype(F32), low.astype(F32)
+    count = x.shape[0]
     for y in range(P_SIZE):
         part = slice(y * 32, y * 32 + 32)
-        rows[pl.ds(y, x.shape[0], stride=P_SIZE), :] = jnp.concatenate([high[:, part], low[:, part]], axis=1)
-    return rows[...].astype(BF16)
+        rows[y * count : y * count + count, :] = jnp.concatenate([high[:, part], low[:, part]], axis=1)
+    found = [rows[pl.ds(k, P_SIZE, stride=count), :] for k in range(count)]
+    return jnp.concatenate(found, axis=0).astype(BF16)
 
 
 def stacked(x, width):
@@ -312,25 +314,13 @@
 
 
 FIRST = ("mu", "wide", "small")
-NEXT = ("small", "xa", "ey", "ex", "later", "scales")
+NEXT = ("xa", "ey", "ex", "later", "scales")
 KEPT = (((2, 256, 128), BF16), ((2, 256, 256), BF16), ((2, 128, 512), BF16), ((2, 192, 256), BF16), ((2, 128, 1408), BF16), ((768, 256), F32))
 
 
-def fetch_kernel(after_ref, *refs):
-    places = {1: lax.axis_index("gs"), 2: lax.axis_index("gy"), 3: lax.axis_index("gc")}
-    n = len(NEXT)
-    copies = [
-        pltpu.make_async_copy(source.at[places[i]] if i in places else source, target, refs[-1].at[i])
-        for i, (source, target) in enumerate(zip(refs[:n], refs[n : 2 * n]))
-    ]
-    for copy in copies:
-        copy.start()
-    for copy in copies:
-        copy.wait()
-
-
-def first_kernel(q_hbm, mu_hbm, wide_hbm, small_hbm, m_ref, own_ref, spec_ref,
-                 q, mu, wide, small, rows, rows32, ls, lp, ly, spill, sem):
+def first_kernel(q_hbm, mu_hbm, wide_hbm, small_hbm, xa_hbm, ey_hbm, ex_hbm, later_hbm, scales_hbm,
+                 m_ref, own_ref, spec_ref, small, xa, ey, ex, later, scales,
+                 q, mu, wide, rows, rows32, sem):
     started = []
 
     def start(source, target):
@@ -342,13 +332,23 @@
     def part(first, last):
         return start(wide_hbm.at[:, first:last, :], wide.at[:, first:last, :])
 
-    now = [start(q_hbm, q), start(small_hbm, small), part(0, 512), start(mu_hbm, mu)]
+    now = [start(q_hbm, q), start(small_hbm, small)]
+    soon = [part(0, 512), start(mu_hbm, mu)]
     for copy in now:
         copy.wait()
-    soon = [part(512, 1536), part(1536, 2560)]
+    late = [part(512, 1536), part(1536, 2560)]
     t = {name: View(wide, *place) for name, place in WIDE.items()}
     x = row_times(small_table(small, "sc|"), q[...])
     x = block_times_nt(small_table(small, "sc="), spread(x, rows))
+    for copy in soon:
+        copy.wait()
+    ahead = [
+        start(xa_hbm.at[lax.axis_index("gs")], xa),
+        start(ey_hbm.at[lax.axis_index("gy")], ey),
+        start(ex_hbm.at[lax.axis_index("gc")], ex),
+        start(scales_hbm, scales),
+        start(later_hbm, later),
+    ]
     x = times_table(stacked(x, 128), t["bd"])
     bd32 = View(small, 128, 128, 0, 128)
     y = row_times(small_table(small, "s32|"), q[...])
@@ -356,24 +356,29 @@
     spec_ref[...] = times_table(stacked(y, 128), bd32)
     x = jnp.concatenate([x[i * 64 : i * 64 + 64] / (mu[16:80, :] + mu[i : i + 1, :]) for i in range(16)], axis=0)
     x = times_table(x, t["ty"])
+    lane = lanes(16)
+    ls, lp, ly = [], [], []
     for i in range(4):
         z = table_times(t["tz"], x[i * 256 : i * 256 + 256])
+        for j in range(0, 4, 2):
+            one, two = z[j * 32 : j * 32 + 32, 0:128], z[j * 32 + 32 : j * 32 + 64, 0:128]
+            ls.append(jnp.where(lane < 64, one[0:16], pltpu.roll(two[0:16], 64, 1)))
+            lp.append(jnp.where(lane < 64, pltpu.roll(one[16:32], 64, 1), two[16:32]))
         for j in range(4):
-            k = i * 4 + j
-            ls[:, k * 64 : k * 64 + 64] = z[j * 32 : j * 32 + 16, 0:64]
-            lp[:, k * 64 : k * 64 + 64] = z[j * 32 + 16 : j * 32 + 32, 64:128]
-            ly[:, k * 16 : k * 16 + 16] = z[j * 32 + 16 : j * 32 + 32, 128:144]
-    for copy in soon:
+            k = (i * 4 + j) % 8
+            one = z[j * 32 + 16 : j * 32 + 32, 128:256]
+            ly.append(pltpu.roll(one, 16 * k, 1) if k else one)
+    ls, lp = jnp.concatenate(ls, axis=1), jnp.concatenate(lp, axis=1)
+    ly = jnp.concatenate([sum(ly[1:8], ly[0]), sum(ly[9:16], ly[8])], axis=1)
+    for copy in late:
         copy.wait()
-    samples = times_table(ls[...], t["tx1"])
-    coefs = times_table(lp[:, 0:512], t["tx2a"]) + times_table(lp[:, 512:1024], t["tx2b"]) + times_table(ly[...], t["tx3"])
+    samples = times_table(ls, t["tx1"])
+    coefs = times_table(lp[:, 0:512], t["tx2a"]) + times_table(lp[:, 512:1024], t["tx2b"]) + times_table(ly, t["tx3"])
     x = row_times(small_table(small, "u|"), samples)
     coefs = coefs - times_table(x[16:32], t["kl"])
     own_ref[...] = coefs
     x = (times_table(x[0:8], t["k1"]) + x[8:16]).T
-    for i in range(16):
-        spill[:, i * 8 : i * 8 + 8] = x[i * 16 : i * 16 + 16]
-    spilled = spill[...]
+    spilled = jnp.concatenate([x[i * 16 : i * 16 + 16] for i in range(16)], axis=1)
     tile = jnp.zeros((8, 128), F32)
     for i in range(8):
         value = coefs[i % 2 * 8 : i % 2 * 8 + 8]
@@ -382,6 +387,8 @@
     for i in range(16):
         m_ref[i * 24 : i * 24 + 16, :] = spilled
         m_ref[i * 24 + 16 : i * 24 + 24, :] = tile
+    for copy in ahead:
+        copy.wait()
 
 
 def unpacked(tile, source, slot):
@@ -435,7 +442,7 @@
     coefs_ref[...] = coefs
 
 
-def last_kernel(m_ref, coefs_ref, spec_ref, small, later, scales, out_ref, rows, flat):
+def last_kernel(m_ref, coefs_ref, spec_ref, small, later, scales, out_ref, rows):
     s32, bd32 = small_table(small, "s32|"), View(small, 128, 128, 0, 128)
     got = jnp.sum(m_ref[...].reshape(16, 8, 128), axis=0)
     coefs = coefs_ref[...] + jnp.where(lax.axis_index("gc") == 0, unpacked(got, 96, 0), unpacked(got, 96, 1))
@@ -452,9 +459,8 @@
     x = times_table(stacked(x, 128), bd32)
     for i in range(8):
         rows[i * 128 : i * 128 + 128, :] = x[i * 32 : i * 32 + 32].T
-    for y in range(P_SIZE):
-        flat[:, y * 32 : y * 32 + 32] = rows[pl.ds(y, 32, stride=P_SIZE), :]
-    out_ref[...] = row_times(s32, flat[...])
+    x = jnp.concatenate([rows[pl.ds(y, 32, stride=P_SIZE), :] for y in range(P_SIZE)], axis=1)
+    out_ref[...] = row_times(s32, x)
 
 
 def vmem(count):
@@ -475,36 +481,22 @@
 
 def body(charge):
     t = {k: pltpu.with_memory_space_constraint(jnp.asarray(v), pltpu.HBM) for k, v in packs().items()}
-    message, own, spec = pl.pallas_call(
+    message, own, spec, small, xa, ey, ex, later, scales = pl.pallas_call(
         first_kernel,
-        out_shape=[shape(384, 128), shape(NL, 128), shape(256, 128)],
-        in_specs=hbm(4),
-        out_specs=vmem(3),
+        out_shape=[shape(384, 128), shape(NL, 128), shape(256, 128)] + [jax.ShapeDtypeStruct(*k) for k in KEPT],
+        in_specs=hbm(1 + len(FIRST) + len(NEXT)),
+        out_specs=vmem(3 + len(KEPT)),
         scratch_shapes=[
             pltpu.VMEM((32, 1024), F32),
             pltpu.VMEM((80, 256), F32),
             pltpu.VMEM((2, 2560, 256), BF16),
-            pltpu.VMEM((2, 256, 128), BF16),
             pltpu.VMEM((2048, 64), F32),
             pltpu.VMEM((1024, 64), F32),
-            pltpu.VMEM((16, 1024), F32),
-            pltpu.VMEM((16, 1024), F32),
-            pltpu.VMEM((16, 256), F32),
-            pltpu.VMEM((16, 128), F32),
-            pltpu.SemaphoreType.DMA((6,)),
+            pltpu.SemaphoreType.DMA((11,)),
         ],
         compiler_params=params(24),
         name="first",
-    )(pltpu.with_memory_space_constraint(charge, pltpu.HBM), *[t[k] for k in FIRST])
-    small, xa, ey, ex, later, scales = pl.pallas_call(
-        fetch_kernel,
-        out_shape=[jax.ShapeDtypeStruct(*k) for k in KEPT],
-        in_specs=hbm(1 + len(NEXT)),
-        out_specs=vmem(len(KEPT)),
-        scratch_shapes=[pltpu.SemaphoreType.DMA((len(NEXT),))],
-        compiler_params=params(12),
-        name="fetch",
-    )(own, *[t[k] for k in NEXT])
+    )(pltpu.with_memory_space_constraint(charge, pltpu.HBM), *[t[k] for k in FIRST + NEXT])
     strip = lax.all_to_all(message.reshape(16, 24, 128), ("gc", "gy"), 0, 0).reshape(384, 128)
     message, coefs = pl.pallas_call(
         strip_kernel,
@@ -520,7 +512,7 @@
         out_shape=shape(32, 1024),
         in_specs=vmem(6),
         out_specs=vmem(1)[0],
-        scratch_shapes=[pltpu.VMEM((1024, 32), F32), pltpu.VMEM((32, 1024), F32)],
+        scratch_shapes=[pltpu.VMEM((1024, 32), F32)],
         compiler_params=params(12),
         name="last",
     )(arrived, coefs, spec, small, later, scales)

time: 42.3 us -> 41.9 us (level)
  blocking collectives: 19.4 us -> 32.7 us
  starting transfers between devices: 6.84 us -> 0 us
  waiting for transfers between devices: 4.95 us -> 0 us
  Pallas kernels: 10.9 us -> 8.99 us
    all_to_all x0 -> x1, blocking collectives: none -> 13.3 us  [body(): lax.all_to_all(message.reshape(16, 24, 128), ('gc', 'gy'), 0, 0)]
    all_to_all x1 -> x0, starting transfers between devices: 6.84 us -> none  [body(): lax.all_to_all(message.reshape(16, 24, 128), ('gc', 'gy'), 0, 0)]
    all_to_all x1 -> x0, waiting for transfers between devices: 4.95 us -> none  [body(): lax.all_to_all(message.reshape(16, 24, 128), ('gc', 'gy'), 0, 0)]
    pallas_call x1 -> x0, Pallas kernels: 1.7 us -> none  [body(): pl.pallas_call(fetch_kernel, out_shape=[jax.ShapeDtypeStruct(*k) for k in...]
  transfers between devices with their start and end apart: 1 -> 0, of which waited for: 1 -> 0; matrix products, arithmetic and copies ran while one was open for 0% -> 0% of each run, Pallas kernels for 4% -> 0%
where the time goes in v4:
time: 41.9 us; the launch traced here: 41.7 us
  blocking collectives  32.7 us (78%)
  Pallas kernels  8.99 us (21%)
    all_to_all x1, blocking collectives, body(): lax.all_to_all(message.reshape(16, 8, 128), 'gs', 0, 0).reshape(128, 128)  19.4 us
    all_to_all x1, blocking collectives, body(): lax.all_to_all(message.reshape(16, 24, 128), ('gc', 'gy'), 0, 0)  13.3 us
    pallas_call x1, Pallas kernels, body(): pl.pallas_call(first_kernel, out_shape=[shape(384, 128), shape(NL, 128),...  5.69 us
    pallas_call x1, Pallas kernels, body(): pl.pallas_call(last_kernel, out_shape=shape(32, 1024), in_specs=vmem(6),...  1.95 us
    pallas_call x1, Pallas kernels, body(): pl.pallas_call(strip_kernel, out_shape=(shape(128, 128), shape(NL, 128)),...  1.35 us

profile of v4, /device:TPU:1, one launch (start us, length us, event | category | flops | bytes accessed | tf_op | source)
XLA Modules:
  0.0 41.7 jit_solution(76548379481833360)
XLA Ops:
  0.0 5.7 %first.1 = (f32[384,128]{1,0:T(8,128)S(1)}, f32[16,128]{1,0:T(8,128)S(1)}, f32[256,128]{1,0:T(8,128)S(1)}, bf16[2,256,128]{2,1,0:T(8,128)(2,1)S(1)}, bf16[2,256,...) custom-call(f32[32,1024]{1,0:T(8,128)} %q_hbm.1, ...), custom_call_target="tpu_custom_call" | custom-call | tf_op jit(solution)/shard_map/first/pallas_call | solution.py:484
  5.7 13.3 %all_to_all.10 = f32[16,24,128]{2,1,0:T(8,128)S(1)} all-to-all(f32[16,24,128]{2,1,0:T(8,128)S(1)} %bitcast.6), channel_id=1, replica_groups=mesh['gs'=16,'gc'=2,'gy'=8] {'gc','gy'}, dimensions={0} | all-to-all | bytes 393216 | tf_op jit(solution)/shard_map/all_to_all | solution.py:500
  19.0 1.4 %strip.1 = (f32[128,128]{1,0:T(8,128)S(1)}, f32[16,128]{1,0:T(8,128)S(1)}) custom-call(f32[384,128]{1,0:T(8,128)S(1)} %bitcast.4, f32[16,128]{1,0:T(8,128)S(1)} %get-tuple-element.17.own_ref, bf16[2,256,256]{2,1,0:T(8,128)(2,1)S(1)} %get-tuple-element.18.xa, bf16[2,128,512]{2,1,0:T(8,128)(2,1)S(1)} %get-tuple-element.19.ey, ...), custom_call_target="tpu_custom_call" | custom-call | tf_op jit(solution)/shard_map/strip/pallas_call | solution.py:501
  20.3 19.4 %all_to_all.11 = f32[16,8,128]{2,1,0:T(8,128)S(1)} all-to-all(f32[16,8,128]{2,1,0:T(8,128)S(1)} %bitcast.7), channel_id=1, replica_groups=mesh['gs'=16,'gc'=2,'gy'=8] {'gs'}, dimensions={0} | all-to-all | bytes 131072 | tf_op jit(solution)/shard_map/all_to_all | solution.py:509
  39.7 2.0 %last.1 = f32[32,1024]{1,0:T(8,128)} custom-call(f32[128,128]{1,0:T(8,128)S(1)} %bitcast.5, f32[16,128]{1,0:T(8,128)S(1)} %get-tuple-element.24.coefs_ref, f32[256,128]{1,0:T(8,128)S(1)} %get-tuple-element.25.spec_ref, bf16[2,256,128]{2,1,0:T(8,128)(2,1)S(1)} %get-tuple-element.26.small, bf16[2,128,1408]{2,1,0:T(8,128)(2,1)S(1)} %get-tuple-element.21.later, ...), custom_call_target="tpu_custom_call" | custom-call | tf_op jit(solution)/shard_map/last/pallas_call | solution.py:510

commit v5 on v4

--- a/solution.py
+++ b/solution.py
@@ -296,8 +296,8 @@
     count = x.shape[0]
     for y in range(P_SIZE):
         part = slice(y * 32, y * 32 + 32)
-        rows[y * count : y * count + count, :] = jnp.concatenate([high[:, part], low[:, part]], axis=1)
-    found = [rows[pl.ds(k, P_SIZE, stride=count), :] for k in range(count)]
+        rows[y * (count + 1) : y * (count + 1) + count, :] = jnp.concatenate([high[:, part], low[:, part]], axis=1)
+    found = [rows[pl.ds(k, P_SIZE, stride=count + 1), :] for k in range(count)]
     return jnp.concatenate(found, axis=0).astype(BF16)
 
 
@@ -337,11 +337,6 @@
     for copy in now:
         copy.wait()
     late = [part(512, 1536), part(1536, 2560)]
-    t = {name: View(wide, *place) for name, place in WIDE.items()}
-    x = row_times(small_table(small, "sc|"), q[...])
-    x = block_times_nt(small_table(small, "sc="), spread(x, rows))
-    for copy in soon:
-        copy.wait()
     ahead = [
         start(xa_hbm.at[lax.axis_index("gs")], xa),
         start(ey_hbm.at[lax.axis_index("gy")], ey),
@@ -349,6 +344,11 @@
         start(scales_hbm, scales),
         start(later_hbm, later),
     ]
+    t = {name: View(wide, *place) for name, place in WIDE.items()}
+    x = row_times(small_table(small, "sc|"), q[...])
+    x = block_times_nt(small_table(small, "sc="), spread(x, rows))
+    for copy in soon:
+        copy.wait()
     x = times_table(stacked(x, 128), t["bd"])
     bd32 = View(small, 128, 128, 0, 128)
     y = row_times(small_table(small, "s32|"), q[...])
@@ -458,8 +458,10 @@
     x = row_times(s32, unstacked(x, 32))
     x = times_table(stacked(x, 128), bd32)
     for i in range(8):
-        rows[i * 128 : i * 128 + 128, :] = x[i * 32 : i * 32 + 32].T
-    x = jnp.concatenate([rows[pl.ds(y, 32, stride=P_SIZE), :] for y in range(P_SIZE)], axis=1)
+        turned = x[i * 32 : i * 32 + 32].T
+        for j in range(4):
+            rows[(i * 4 + j) * 33 : (i * 4 + j) * 33 + 32, :] = turned[j * 32 : j * 32 + 32]
+    x = jnp.concatenate([rows[pl.ds(y, 32, stride=P_SIZE + 1), :] for y in range(P_SIZE)], axis=1)
     out_ref[...] = row_times(s32, x)
 
 
@@ -490,8 +492,8 @@
             pltpu.VMEM((32, 1024), F32),
             pltpu.VMEM((80, 256), F32),
             pltpu.VMEM((2, 2560, 256), BF16),
-            pltpu.VMEM((2048, 64), F32),
-            pltpu.VMEM((1024, 64), F32),
+            pltpu.VMEM((2080, 64), F32),
+            pltpu.VMEM((1056, 64), F32),
             pltpu.SemaphoreType.DMA((11,)),
         ],
         compiler_params=params(24),
@@ -512,7 +514,7 @@
         out_shape=shape(32, 1024),
         in_specs=vmem(6),
         out_specs=vmem(1)[0],
-        scratch_shapes=[pltpu.VMEM((1024, 32), F32)],
+        scratch_shapes=[pltpu.VMEM((1056, 32), F32)],
         compiler_params=params(12),
         name="last",
     )(arrived, coefs, spec, small, later, scales)

time: 41.9 us -> 40.7 us (0.971)
  Pallas kernels: 8.99 us -> 7.79 us
    pallas_call x1, Pallas kernels: 5.69 us -> 4.59 us  [body(): pl.pallas_call(first_kernel, out_shape=[shape(384, 128), shape(NL, 128),...]
where the time goes in v5:
time: 40.7 us; the launch traced here: 40.5 us
  blocking collectives  32.7 us (80%)
  Pallas kernels  7.79 us (19%)
    all_to_all x1, blocking collectives, body(): lax.all_to_all(message.reshape(16, 8, 128), 'gs', 0, 0).reshape(128, 128)  19.4 us
    all_to_all x1, blocking collectives, body(): lax.all_to_all(message.reshape(16, 24, 128), ('gc', 'gy'), 0, 0)  13.3 us
    pallas_call x1, Pallas kernels, body(): pl.pallas_call(first_kernel, out_shape=[shape(384, 128), shape(NL, 128),...  4.59 us
    pallas_call x1, Pallas kernels, body(): pl.pallas_call(last_kernel, out_shape=shape(32, 1024), in_specs=vmem(6),...  1.85 us
    pallas_call x1, Pallas kernels, body(): pl.pallas_call(strip_kernel, out_shape=(shape(128, 128), shape(NL, 128)),...  1.35 us

profile of v5, /device:TPU:1, one launch (start us, length us, event | category | flops | bytes accessed | tf_op | source)
XLA Modules:
  0.0 40.5 jit_solution(4129142067835858759)
XLA Ops:
  0.0 4.6 %first.1 = (f32[384,128]{1,0:T(8,128)S(1)}, f32[16,128]{1,0:T(8,128)S(1)}, f32[256,128]{1,0:T(8,128)S(1)}, bf16[2,256,128]{2,1,0:T(8,128)(2,1)S(1)}, bf16[2,256,...) custom-call(f32[32,1024]{1,0:T(8,128)} %q_hbm.1, ...), custom_call_target="tpu_custom_call" | custom-call | tf_op jit(solution)/shard_map/first/pallas_call | solution.py:486
  4.6 13.3 %all_to_all.10 = f32[16,24,128]{2,1,0:T(8,128)S(1)} all-to-all(f32[16,24,128]{2,1,0:T(8,128)S(1)} %bitcast.6), channel_id=1, replica_groups=mesh['gs'=16,'gc'=2,'gy'=8] {'gc','gy'}, dimensions={0} | all-to-all | bytes 393216 | tf_op jit(solution)/shard_map/all_to_all | solution.py:502
  17.9 1.4 %strip.1 = (f32[128,128]{1,0:T(8,128)S(1)}, f32[16,128]{1,0:T(8,128)S(1)}) custom-call(f32[384,128]{1,0:T(8,128)S(1)} %bitcast.4, f32[16,128]{1,0:T(8,128)S(1)} %get-tuple-element.17.own_ref, bf16[2,256,256]{2,1,0:T(8,128)(2,1)S(1)} %get-tuple-element.18.xa, bf16[2,128,512]{2,1,0:T(8,128)(2,1)S(1)} %get-tuple-element.19.ey, ...), custom_call_target="tpu_custom_call" | custom-call | tf_op jit(solution)/shard_map/strip/pallas_call | solution.py:503
  19.2 19.4 %all_to_all.11 = f32[16,8,128]{2,1,0:T(8,128)S(1)} all-to-all(f32[16,8,128]{2,1,0:T(8,128)S(1)} %bitcast.7), channel_id=1, replica_groups=mesh['gs'=16,'gc'=2,'gy'=8] {'gs'}, dimensions={0} | all-to-all | bytes 131072 | tf_op jit(solution)/shard_map/all_to_all | solution.py:511
  38.6 1.8 %last.1 = f32[32,1024]{1,0:T(8,128)} custom-call(f32[128,128]{1,0:T(8,128)S(1)} %bitcast.5, f32[16,128]{1,0:T(8,128)S(1)} %get-tuple-element.24.coefs_ref, f32[256,128]{1,0:T(8,128)S(1)} %get-tuple-element.25.spec_ref, bf16[2,256,128]{2,1,0:T(8,128)(2,1)S(1)} %get-tuple-element.26.small, bf16[2,128,1408]{2,1,0:T(8,128)(2,1)S(1)} %get-tuple-element.21.later, ...), custom_call_target="tpu_custom_call" | custom-call | tf_op jit(solution)/shard_map/last/pallas_call | solution.py:512

commit v6 on v5

--- a/solution.py
+++ b/solution.py
@@ -338,11 +338,11 @@
         copy.wait()
     late = [part(512, 1536), part(1536, 2560)]
     ahead = [
+        start(scales_hbm, scales),
+        start(later_hbm, later),
         start(xa_hbm.at[lax.axis_index("gs")], xa),
         start(ey_hbm.at[lax.axis_index("gy")], ey),
         start(ex_hbm.at[lax.axis_index("gc")], ex),
-        start(scales_hbm, scales),
-        start(later_hbm, later),
     ]
     t = {name: View(wide, *place) for name, place in WIDE.items()}
     x = row_times(small_table(small, "sc|"), q[...])
@@ -411,29 +411,27 @@
     x = times_table(x, xa) * scales[0:512, :]
     x = table_times(ey, x)
     x = table_times(ex, x, dot_nt)
-    m_ref[...] = jnp.zeros((128, 128), F32)
+
+    def tile_of(i, j):
+        return got_ref[pl.ds(pl.multiple_of((i * 8 + j) * 24 + 16, 8), 8), :]
+
+    partner = tile_of(1 - c, b)
+    outside = jnp.where(c == 0, pltpu.roll(partner, 64, 1), pltpu.roll(partner, 96, 1))
+    outside = jnp.where(lanes(8) >= 96, outside, 0.0)
+    fifth = outside[7:8]
+    for j in range(3):
+        fifth = fifth + pltpu.roll(outside, 32 * j + 32, 1)[4 + j : 5 + j]
+    hit = lax.broadcasted_iota(jnp.int32, (16, 128), 0) == s + 1 - 2 * c
     lane = lanes(16)
     for f in range(2):
-        m_ref[pl.ds(f, 16, stride=8), :] = jnp.where(lane < 80, x[160 + f * 16 : 176 + f * 16], 0.0)
+        value = jnp.where(lane < 80, x[160 + f * 16 : 176 + f * 16], 0.0)
+        m_ref[pl.ds(f, 16, stride=5), :] = value + jnp.where(hit, outside[f : f + 1], 0.0)
         value = jnp.zeros((16, 128), F32)
         for k in range(CELLS + 2):
             part = pltpu.roll(x[k * 16 : k * 16 + 16], (8 * (k - 10 - f)) % 128, 1)
             value = jnp.where(lane // 8 == k, part, value)
-        m_ref[pl.ds(2 + f, 16, stride=8), :] = value
-
-    def tile_of(i, j):
-        return got_ref[pl.ds(pl.multiple_of((i * 8 + j) * 24 + 16, 8), 8), :]
-
-    partner = tile_of(1 - c, b)
-    outside = jnp.where(c == 0, pltpu.roll(partner, 64, 1), pltpu.roll(partner, 96, 1))
-    outside = jnp.where(lanes(8) >= 96, outside, 0.0)
-    target = s + 1 - 2 * c
-
-    @pl.when((target >= 0) & (target < 16))
-    def _():
-        where = pl.ds(pl.multiple_of(target * 8, 8), 8)
-        m_ref[where, :] = m_ref[where, :] + outside
-
+        m_ref[pl.ds(2 + f, 16, stride=5), :] = value + jnp.where(hit, outside[2 + f : 3 + f], 0.0)
+    m_ref[pl.ds(4, 16, stride=5), :] = jnp.where(hit, fifth, 0.0)
     coefs = jnp.where(lane < 64, own_ref[...], 0.0)
     coefs = coefs + jnp.where(c == 0, unpacked(partner, 0, 1), unpacked(partner, 32, 0))
     above = unpacked(tile_of(c, jnp.minimum(b + 1, N_GY - 1)), 64, 3)
@@ -444,10 +442,12 @@
 
 def last_kernel(m_ref, coefs_ref, spec_ref, small, later, scales, out_ref, rows):
     s32, bd32 = small_table(small, "s32|"), View(small, 128, 128, 0, 128)
-    got = jnp.sum(m_ref[...].reshape(16, 8, 128), axis=0)
-    coefs = coefs_ref[...] + jnp.where(lax.axis_index("gc") == 0, unpacked(got, 96, 0), unpacked(got, 96, 1))
+    got = [jnp.sum(m_ref[pl.ds(i, 16, stride=5), :], axis=0, keepdims=True) for i in range(5)]
+    tile = got[:4] + [pltpu.roll(got[4], 96 - 32 * j, 1) if j < 3 else got[4] for j in range(4)]
+    tile = jnp.concatenate(tile, axis=0)
+    coefs = coefs_ref[...] + jnp.where(lax.axis_index("gc") == 0, unpacked(tile, 96, 0), unpacked(tile, 96, 1))
     lz = scales[512:544, 128:256]
-    high, low = split(jnp.concatenate([lz * got[i : i + 1] for i in range(4)], axis=1))
+    high, low = split(jnp.concatenate([lz * got[i] for i in range(4)], axis=1))
     x = row_times(later[0, 64:96, 1024:1072], coefs)
     for i in range(4):
         part = jnp.concatenate([high[:, i * 128 : i * 128 + 128], low[:, i * 128 : i * 128 + 128]], axis=0)
@@ -502,13 +502,13 @@
     strip = lax.all_to_all(message.reshape(16, 24, 128), ("gc", "gy"), 0, 0).reshape(384, 128)
     message, coefs = pl.pallas_call(
         strip_kernel,
-        out_shape=(shape(128, 128), shape(NL, 128)),
+        out_shape=(shape(80, 128), shape(NL, 128)),
         in_specs=vmem(7),
         out_specs=tuple(vmem(2)),
         compiler_params=params(12),
         name="strip",
     )(strip, own, xa, ey, ex, later, scales)
-    arrived = lax.all_to_all(message.reshape(16, 8, 128), "gs", 0, 0).reshape(128, 128)
+    arrived = lax.all_to_all(message.reshape(16, 1, 640), "gs", 0, 0).reshape(80, 128)
     return pl.pallas_call(
         last_kernel,
         out_shape=shape(32, 1024),

time: 40.7 us -> 40.6 us (level)
  no operation moved by 1% of the time
where the time goes in v6:
time: 40.6 us; the launch traced here: 40.5 us
  blocking collectives  32.7 us (81%)
  Pallas kernels  7.77 us (19%)
    all_to_all x1, blocking collectives, body(): lax.all_to_all(message.reshape(16, 1, 640), 'gs', 0, 0).reshape(80, 128)  19.4 us
    all_to_all x1, blocking collectives, body(): lax.all_to_all(message.reshape(16, 24, 128), ('gc', 'gy'), 0, 0)  13.3 us
    pallas_call x1, Pallas kernels, body(): pl.pallas_call(first_kernel, out_shape=[shape(384, 128), shape(NL, 128),...  4.59 us
    pallas_call x1, Pallas kernels, body(): pl.pallas_call(last_kernel, out_shape=shape(32, 1024), in_specs=vmem(6),...  1.91 us
    pallas_call x1, Pallas kernels, body(): pl.pallas_call(strip_kernel, out_shape=(shape(80, 128), shape(NL, 128)),...  1.27 us

profile of v6, /device:TPU:1, one launch (start us, length us, event | category | flops | bytes accessed | tf_op | source)
XLA Modules:
  0.0 40.5 jit_solution(7262943521964119611)
XLA Ops:
  0.0 4.6 %first.1 = (f32[384,128]{1,0:T(8,128)S(1)}, f32[16,128]{1,0:T(8,128)S(1)}, f32[256,128]{1,0:T(8,128)S(1)}, bf16[2,256,128]{2,1,0:T(8,128)(2,1)S(1)}, bf16[2,256,...) custom-call(f32[32,1024]{1,0:T(8,128)} %q_hbm.1, ...), custom_call_target="tpu_custom_call" | custom-call | tf_op jit(solution)/shard_map/first/pallas_call | solution.py:486
  4.6 13.3 %all_to_all.10 = f32[16,24,128]{2,1,0:T(8,128)S(1)} all-to-all(f32[16,24,128]{2,1,0:T(8,128)S(1)} %bitcast.5), channel_id=1, replica_groups=mesh['gs'=16,'gc'=2,'gy'=8] {'gc','gy'}, dimensions={0} | all-to-all | bytes 393216 | tf_op jit(solution)/shard_map/all_to_all | solution.py:502
  17.9 1.3 %strip.1 = (f32[80,128]{1,0:T(8,128)S(1)}, f32[16,128]{1,0:T(8,128)S(1)}) custom-call(f32[384,128]{1,0:T(8,128)S(1)} %bitcast.4, f32[16,128]{1,0:T(8,128)S(1)} %get-tuple-element.17.own_ref, bf16[2,256,256]{2,1,0:T(8,128)(2,1)S(1)} %get-tuple-element.18.xa, bf16[2,128,512]{2,1,0:T(8,128)(2,1)S(1)} %get-tuple-element.19.ey, ...), custom_call_target="tpu_custom_call" | custom-call | tf_op jit(solution)/shard_map/strip/pallas_call | solution.py:503
  19.2 19.4 %all_to_all.11 = f32[16,1,640]{2,1,0:T(1,128)S(1)} all-to-all(f32[16,1,640]{2,1,0:T(1,128)S(1)} %bitcast.7), channel_id=1, replica_groups=mesh['gs'=16,'gc'=2,'gy'=8] {'gs'}, dimensions={0} | all-to-all | bytes 81920 | tf_op jit(solution)/shard_map/all_to_all | solution.py:511
  38.5 1.9 %last.1 = f32[32,1024]{1,0:T(8,128)} custom-call(f32[80,128]{1,0:T(8,128)S(1)} %bitcast.6, f32[16,128]{1,0:T(8,128)S(1)} %get-tuple-element.24.coefs_ref, f32[256,128]{1,0:T(8,128)S(1)} %get-tuple-element.25.spec_ref, bf16[2,256,128]{2,1,0:T(8,128)(2,1)S(1)} %get-tuple-element.26.small, bf16[2,128,1408]{2,1,0:T(8,128)(2,1)S(1)} %get-tuple-element.21.later, ...), custom_call_target="tpu_custom_call" | custom-call | tf_op jit(solution)/shard_map/last/pallas_call | solution.py:512

commit v7 on v6

--- a/solution.py
+++ b/solution.py
@@ -190,7 +190,7 @@
     "tx3": (2304, 256, 0, 128),
     "kl": (2304, 256, 128, 128),
 }
-SMALL = {"sc|": (0, 0, 64, 0, 96), "s32|": (0, 64, 32, 0, 96), "u|": (0, 96, 32, 0, 48), "sc=": (1, 0, 128, 0, 64), "s32=": (1, 0, 64, 64, 64)}
+SMALL = {"sc|": (0, 0, 64, 0, 96), "s32|": (0, 64, 32, 0, 96), "u|": (0, 96, 32, 0, 48), "sc=": (1, 0, 64, 0, 96), "s32=": (1, 64, 32, 0, 96)}
 
 
 def in_row(table):
@@ -198,7 +198,7 @@
 
 
 def in_block(table):
-    return np.block([[table[0], table[0]], [table[1], np.zeros_like(table[1])]])
+    return np.concatenate([table[0], table[0], table[1]], axis=1)
 
 
 @functools.lru_cache(None)
@@ -285,9 +285,7 @@
 
 
 def block_times_nt(table, x):
-    both = dot_nt(table, x)
-    rows = table.shape[0] // 2
-    return both[:rows] + both[rows:]
+    return dot_nt(table, x)
 
 
 def spread(x, rows):
@@ -296,7 +294,7 @@
     count = x.shape[0]
     for y in range(P_SIZE):
         part = slice(y * 32, y * 32 + 32)
-        rows[y * (count + 1) : y * (count + 1) + count, :] = jnp.concatenate([high[:, part], low[:, part]], axis=1)
+        rows[y * (count + 1) : y * (count + 1) + count, :] = jnp.concatenate([high[:, part], low[:, part], high[:, part]], axis=1)
     found = [rows[pl.ds(k, P_SIZE, stride=count + 1), :] for k in range(count)]
     return jnp.concatenate(found, axis=0).astype(BF16)
 
@@ -440,7 +438,7 @@
     coefs_ref[...] = coefs
 
 
-def last_kernel(m_ref, coefs_ref, spec_ref, small, later, scales, out_ref, rows):
+def last_kernel(m_ref, coefs_ref, spec_ref, small, later, scales, out_ref, rows, done, sem):
     s32, bd32 = small_table(small, "s32|"), View(small, 128, 128, 0, 128)
     got = [jnp.sum(m_ref[pl.ds(i, 16, stride=5), :], axis=0, keepdims=True) for i in range(5)]
     tile = got[:4] + [pltpu.roll(got[4], 96 - 32 * j, 1) if j < 3 else got[4] for j in range(4)]
@@ -462,7 +460,13 @@
         for j in range(4):
             rows[(i * 4 + j) * 33 : (i * 4 + j) * 33 + 32, :] = turned[j * 32 : j * 32 + 32]
     x = jnp.concatenate([rows[pl.ds(y, 32, stride=P_SIZE + 1), :] for y in range(P_SIZE)], axis=1)
-    out_ref[...] = row_times(s32, x)
+    copies = []
+    for i in range(4):
+        done[:, i * 256 : i * 256 + 256] = row_times(s32, x[:, i * 256 : i * 256 + 256])
+        copies.append(pltpu.make_async_copy(done.at[:, i * 256 : i * 256 + 256], out_ref.at[:, i * 256 : i * 256 + 256], sem.at[i]))
+        copies[-1].start()
+    for copy in copies:
+        copy.wait()
 
 
 def vmem(count):
@@ -492,8 +496,8 @@
             pltpu.VMEM((32, 1024), F32),
             pltpu.VMEM((80, 256), F32),
             pltpu.VMEM((2, 2560, 256), BF16),
-            pltpu.VMEM((2080, 64), F32),
-            pltpu.VMEM((1056, 64), F32),
+            pltpu.VMEM((2080, 96), F32),
+            pltpu.VMEM((1056, 96), F32),
             pltpu.SemaphoreType.DMA((11,)),
         ],
         compiler_params=params(24),
@@ -513,8 +517,8 @@
         last_kernel,
         out_shape=shape(32, 1024),
         in_specs=vmem(6),
-        out_specs=vmem(1)[0],
-        scratch_shapes=[pltpu.VMEM((1056, 32), F32)],
+        out_specs=hbm(1)[0],
+        scratch_shapes=[pltpu.VMEM((1056, 32), F32), pltpu.VMEM((32, 1024), F32), pltpu.SemaphoreType.DMA((4,))],
         compiler_params=params(12),
         name="last",
     )(arrived, coefs, spec, small, later, scales)

time: 40.6 us -> 40.6 us (level)
  no operation moved by 1% of the time
where the time goes in v7:
time: 40.6 us; the launch traced here: 40.4 us
  blocking collectives  32.7 us (81%)
  Pallas kernels  7.74 us (19%)
    all_to_all x1, blocking collectives, body(): lax.all_to_all(message.reshape(16, 1, 640), 'gs', 0, 0).reshape(80, 128)  19.4 us
    all_to_all x1, blocking collectives, body(): lax.all_to_all(message.reshape(16, 24, 128), ('gc', 'gy'), 0, 0)  13.3 us
    pallas_call x1, Pallas kernels, body(): pl.pallas_call(first_kernel, out_shape=[shape(384, 128), shape(NL, 128),...  4.57 us
    pallas_call x1, Pallas kernels, body(): pl.pallas_call(last_kernel, out_shape=shape(32, 1024), in_specs=vmem(6),...  1.9 us
    pallas_call x1, Pallas kernels, body(): pl.pallas_call(strip_kernel, out_shape=(shape(80, 128), shape(NL, 128)),...  1.27 us

profile of v7, /device:TPU:1, one launch (start us, length us, event | category | flops | bytes accessed | tf_op | source)
XLA Modules:
  0.0 40.4 jit_solution(1411130273912121898)
XLA Ops:
  0.0 4.6 %first.1 = (f32[384,128]{1,0:T(8,128)S(1)}, f32[16,128]{1,0:T(8,128)S(1)}, f32[256,128]{1,0:T(8,128)S(1)}, bf16[2,256,128]{2,1,0:T(8,128)(2,1)S(1)}, bf16[2,256,...) custom-call(f32[32,1024]{1,0:T(8,128)} %q_hbm.1, ...), custom_call_target="tpu_custom_call" | custom-call | tf_op jit(solution)/shard_map/first/pallas_call | solution.py:490
  4.6 13.3 %all_to_all.10 = f32[16,24,128]{2,1,0:T(8,128)S(1)} all-to-all(f32[16,24,128]{2,1,0:T(8,128)S(1)} %bitcast.5), channel_id=1, replica_groups=mesh['gs'=16,'gc'=2,'gy'=8] {'gc','gy'}, dimensions={0} | all-to-all | bytes 393216 | tf_op jit(solution)/shard_map/all_to_all | solution.py:506
  17.9 1.3 %strip.1 = (f32[80,128]{1,0:T(8,128)S(1)}, f32[16,128]{1,0:T(8,128)S(1)}) custom-call(f32[384,128]{1,0:T(8,128)S(1)} %bitcast.4, f32[16,128]{1,0:T(8,128)S(1)} %get-tuple-element.17.own_ref, bf16[2,256,256]{2,1,0:T(8,128)(2,1)S(1)} %get-tuple-element.18.xa, bf16[2,128,512]{2,1,0:T(8,128)(2,1)S(1)} %get-tuple-element.19.ey, ...), custom_call_target="tpu_custom_call" | custom-call | tf_op jit(solution)/shard_map/strip/pallas_call | solution.py:507
  19.1 19.4 %all_to_all.11 = f32[16,1,640]{2,1,0:T(1,128)S(1)} all-to-all(f32[16,1,640]{2,1,0:T(1,128)S(1)} %bitcast.7), channel_id=1, replica_groups=mesh['gs'=16,'gc'=2,'gy'=8] {'gs'}, dimensions={0} | all-to-all | bytes 81920 | tf_op jit(solution)/shard_map/all_to_all | solution.py:515
  38.5 1.9 %last.1 = f32[32,1024]{1,0:T(8,128)} custom-call(f32[80,128]{1,0:T(8,128)S(1)} %bitcast.6, f32[16,128]{1,0:T(8,128)S(1)} %get-tuple-element.24.coefs_ref, f32[256,128]{1,0:T(8,128)S(1)} %get-tuple-element.25.spec_ref, bf16[2,256,128]{2,1,0:T(8,128)(2,1)S(1)} %get-tuple-element.26.small, bf16[2,128,1408]{2,1,0:T(8,128)(2,1)S(1)} %get-tuple-element.21.later, ...), custom_call_target="tpu_custom_call" | custom-call | tf_op jit(solution)/shard_map/last/pallas_call | solution.py:516

commit v8 on v7

--- a/solution.py
+++ b/solution.py
@@ -334,7 +334,6 @@
     soon = [part(0, 512), start(mu_hbm, mu)]
     for copy in now:
         copy.wait()
-    late = [part(512, 1536), part(1536, 2560)]
     ahead = [
         start(scales_hbm, scales),
         start(later_hbm, later),
@@ -342,6 +341,7 @@
         start(ey_hbm.at[lax.axis_index("gy")], ey),
         start(ex_hbm.at[lax.axis_index("gc")], ex),
     ]
+    late = [part(512, 1536), part(1536, 2560)]
     t = {name: View(wide, *place) for name, place in WIDE.items()}
     x = row_times(small_table(small, "sc|"), q[...])
     x = block_times_nt(small_table(small, "sc="), spread(x, rows))
@@ -438,7 +438,7 @@
     coefs_ref[...] = coefs
 
 
-def last_kernel(m_ref, coefs_ref, spec_ref, small, later, scales, out_ref, rows, done, sem):
+def last_kernel(m_ref, coefs_ref, spec_ref, small, later, scales, out_ref, rows):
     s32, bd32 = small_table(small, "s32|"), View(small, 128, 128, 0, 128)
     got = [jnp.sum(m_ref[pl.ds(i, 16, stride=5), :], axis=0, keepdims=True) for i in range(5)]
     tile = got[:4] + [pltpu.roll(got[4], 96 - 32 * j, 1) if j < 3 else got[4] for j in range(4)]
@@ -460,13 +460,7 @@
         for j in range(4):
             rows[(i * 4 + j) * 33 : (i * 4 + j) * 33 + 32, :] = turned[j * 32 : j * 32 + 32]
     x = jnp.concatenate([rows[pl.ds(y, 32, stride=P_SIZE + 1), :] for y in range(P_SIZE)], axis=1)
-    copies = []
-    for i in range(4):
-        done[:, i * 256 : i * 256 + 256] = row_times(s32, x[:, i * 256 : i * 256 + 256])
-        copies.append(pltpu.make_async_copy(done.at[:, i * 256 : i * 256 + 256], out_ref.at[:, i * 256 : i * 256 + 256], sem.at[i]))
-        copies[-1].start()
-    for copy in copies:
-        copy.wait()
+    out_ref[...] = row_times(s32, x)
 
 
 def vmem(count):
@@ -517,8 +511,8 @@
         last_kernel,
         out_shape=shape(32, 1024),
         in_specs=vmem(6),
-        out_specs=hbm(1)[0],
-        scratch_shapes=[pltpu.VMEM((1056, 32), F32), pltpu.VMEM((32, 1024), F32), pltpu.SemaphoreType.DMA((4,))],
+        out_specs=vmem(1)[0],
+        scratch_shapes=[pltpu.VMEM((1056, 32), F32)],
         compiler_params=params(12),
         name="last",
     )(arrived, coefs, spec, small, later, scales)

time: 40.6 us -> 40.6 us (level)
  no operation moved by 1% of the time
where the time goes in v8:
time: 40.6 us; the launch traced here: 40.4 us
  blocking collectives  32.7 us (81%)
  Pallas kernels  7.75 us (19%)
    all_to_all x1, blocking collectives, body(): lax.all_to_all(message.reshape(16, 1, 640), 'gs', 0, 0).reshape(80, 128)  19.4 us
    all_to_all x1, blocking collectives, body(): lax.all_to_all(message.reshape(16, 24, 128), ('gc', 'gy'), 0, 0)  13.3 us
    pallas_call x1, Pallas kernels, body(): pl.pallas_call(first_kernel, out_shape=[shape(384, 128), shape(NL, 128),...  4.57 us
    pallas_call x1, Pallas kernels, body(): pl.pallas_call(last_kernel, out_shape=shape(32, 1024), in_specs=vmem(6),...  1.91 us
    pallas_call x1, Pallas kernels, body(): pl.pallas_call(strip_kernel, out_shape=(shape(80, 128), shape(NL, 128)),...  1.27 us

profile of v8, /device:TPU:1, one launch (start us, length us, event | category | flops | bytes accessed | tf_op | source)
XLA Modules:
  0.0 40.4 jit_solution(2305709892024807617)
XLA Ops:
  0.0 4.6 %first.1 = (f32[384,128]{1,0:T(8,128)S(1)}, f32[16,128]{1,0:T(8,128)S(1)}, f32[256,128]{1,0:T(8,128)S(1)}, bf16[2,256,128]{2,1,0:T(8,128)(2,1)S(1)}, bf16[2,256,...) custom-call(f32[32,1024]{1,0:T(8,128)} %q_hbm.1, ...), custom_call_target="tpu_custom_call" | custom-call | tf_op jit(solution)/shard_map/first/pallas_call | solution.py:484
  4.6 13.3 %all_to_all.10 = f32[16,24,128]{2,1,0:T(8,128)S(1)} all-to-all(f32[16,24,128]{2,1,0:T(8,128)S(1)} %bitcast.5), channel_id=1, replica_groups=mesh['gs'=16,'gc'=2,'gy'=8] {'gc','gy'}, dimensions={0} | all-to-all | bytes 393216 | tf_op jit(solution)/shard_map/all_to_all | solution.py:500
  17.9 1.3 %strip.1 = (f32[80,128]{1,0:T(8,128)S(1)}, f32[16,128]{1,0:T(8,128)S(1)}) custom-call(f32[384,128]{1,0:T(8,128)S(1)} %bitcast.4, f32[16,128]{1,0:T(8,128)S(1)} %get-tuple-element.17.own_ref, bf16[2,256,256]{2,1,0:T(8,128)(2,1)S(1)} %get-tuple-element.18.xa, bf16[2,128,512]{2,1,0:T(8,128)(2,1)S(1)} %get-tuple-element.19.ey, ...), custom_call_target="tpu_custom_call" | custom-call | tf_op jit(solution)/shard_map/strip/pallas_call | solution.py:501
  19.1 19.4 %all_to_all.11 = f32[16,1,640]{2,1,0:T(1,128)S(1)} all-to-all(f32[16,1,640]{2,1,0:T(1,128)S(1)} %bitcast.7), channel_id=1, replica_groups=mesh['gs'=16,'gc'=2,'gy'=8] {'gs'}, dimensions={0} | all-to-all | bytes 81920 | tf_op jit(solution)/shard_map/all_to_all | solution.py:509
  38.5 1.9 %last.1 = f32[32,1024]{1,0:T(8,128)} custom-call(f32[80,128]{1,0:T(8,128)S(1)} %bitcast.6, f32[16,128]{1,0:T(8,128)S(1)} %get-tuple-element.24.coefs_ref, f32[256,128]{1,0:T(8,128)S(1)} %get-tuple-element.25.spec_ref, bf16[2,256,128]{2,1,0:T(8,128)(2,1)S(1)} %get-tuple-element.26.small, bf16[2,128,1408]{2,1,0:T(8,128)(2,1)S(1)} %get-tuple-element.21.later, ...), custom_call_target="tpu_custom_call" | custom-call | tf_op jit(solution)/shard_map/last/pallas_call | solution.py:510
